TPU v7x, 32 devices: a whole 2x2x4 slice. The times are simulated.
32 devices in a mesh: tm: 8 (over y, x, core), fsdp: 4 (over z).
Axes of the slice: x: 2, y: 2, z: 4, core: 2. Of those that a mesh axis runs over, the one named last changes fastest.
Arguments:
- frames: bfloat16 [4, 1024, 1024], P('fsdp', 'tm'), may hold values from -6 to 6
- gain_one: float32 [1024], replicated, may hold values from 0.1 to 1.9
- qkv_one: bfloat16 [1024, 3072], P('fsdp'), may hold values from -0.1875 to 0.1875
- out_one: bfloat16 [1024, 1024], P('fsdp'), may hold values from -0.1875 to 0.1875
- gain_two: float32 [1024], replicated, may hold values from 0.1 to 1.9
- qkv_two: bfloat16 [1024, 3072], P('fsdp'), may hold values from -0.1875 to 0.1875
- lengths: int32 [4], P('fsdp'), may hold values from 512 to 1024, as said below
- left_counts: int32 [4], P('fsdp'), may hold values from 0 to 2, as said below
- cotangent: bfloat16 [4, 1024, 1024], P('fsdp', 'tm'), may hold values from -6 to 6
Outputs:
- context: bfloat16 [4, 1024, 1024], P('fsdp', 'tm')
- weight_grad: float32 [1024, 1024], P(('tm', 'fsdp'))
Inputs may be any that keep to these rules, and one draw needn't show every extreme that they name: `lengths`: some utterance is complete in every draw. `left_counts`: in every draw some utterance takes 2 blocks and another none.
All inputs are finite; a program needn't handle non-finite values.
Results may differ from a plain program's by a relative error of at most 0.029.
Values may be sent and summed in bfloat16 or wider, within the bound.
A program may use at most 64 MiB of HBM per device.

v0:
```python
import functools

import jax
import jax.numpy as jnp
from jax import lax
from jax.experimental import pallas as pl
from jax.experimental.pallas import tpu as pltpu
from jax.sharding import PartitionSpec as P

HEADS = 16
LEFT_MAX = 2
RIGHT = 23
CHIPS = 4


def from_behind(block, axis, distance):
    devices = range(lax.axis_size(axis))
    route = [(i - distance, i) for i in devices if i - distance in devices]
    return lax.ppermute(block, axis, route)


def norm_rows(values, gain):
    wide = values.astype(jnp.float32)
    mean = jnp.mean(wide, axis=-1, keepdims=True)
    var = jnp.mean((wide - mean) ** 2, axis=-1, keepdims=True)
    return ((wide - mean) * lax.rsqrt(var + 1e-05) * gain).astype(jnp.bfloat16)


def attend(query, keys, values, allowed, heads):
    rows_q, width = query.shape
    head = width // heads
    scale = 1.0 / head**0.5
    q_heads = query.reshape(rows_q, heads, head)
    k_heads = keys.reshape(keys.shape[0], heads, head)
    v_heads = values.reshape(values.shape[0], heads, head)
    scores = (
        jnp.einsum("qhe,khe->hqk", q_heads, k_heads, preferred_element_type=jnp.float32) * scale
    )
    scores = jnp.where(allowed[None], scores, -1e30)
    top = jnp.max(scores, axis=-1, keepdims=True)
    expo = jnp.exp(scores - top)
    weights = (expo / jnp.sum(expo, axis=-1, keepdims=True)).astype(jnp.bfloat16)
    ctx = jnp.einsum("hqk,khe->qhe", weights, v_heads, preferred_element_type=jnp.float32)
    return ctx.reshape(rows_q, width).astype(jnp.bfloat16)


def add_rows(left, piece):
    return jnp.dot(left, piece, preferred_element_type=jnp.float32)


def on_device(
    frames, gain_one, qkv_one, out_one, gain_two, qkv_two, lengths, left_counts, cotangent
):
    local = frames[0]
    grad_in = cotangent[0]
    fr, width = local.shape
    block = lax.axis_index("tm")
    length = lengths[0]
    count = left_counts[0]
    norm_one = norm_rows(local, gain_one)
    proj = add_rows(norm_one, lax.all_gather(qkv_one, "fsdp", axis=0, tiled=True))
    proj = proj.astype(jnp.bfloat16)
    query = proj[:, :width]
    key_value = proj[:, width:]
    earlier = [from_behind(key_value, "tm", step) for step in range(LEFT_MAX, 0, -1)]
    gathered = jnp.concatenate(earlier + [key_value], axis=0)
    rows = jnp.arange(fr, dtype=jnp.int32)
    cols = jnp.arange((LEFT_MAX + 1) * fr, dtype=jnp.int32)
    tpos = block * fr + rows[:, None]
    spos = (block - LEFT_MAX) * fr + cols[None, :]
    apart = LEFT_MAX - cols[None, :] // fr
    allowed = (spos >= 0) & (spos <= tpos) & (apart <= count) & ((spos < length) | (spos == tpos))
    ctx_one = attend(query, gathered[:, :width], gathered[:, width:], allowed, HEADS)
    out_proj = add_rows(ctx_one, lax.all_gather(out_one, "fsdp", axis=0, tiled=True))
    hidden = (local.astype(jnp.float32) + out_proj).astype(jnp.bfloat16)
    norm_two = norm_rows(hidden, gain_two)
    proj2 = add_rows(norm_two, lax.all_gather(qkv_two, "fsdp", axis=0, tiled=True))
    proj2 = proj2.astype(jnp.bfloat16)
    query2 = proj2[:, :width]
    key_value2 = proj2[:, width:]
    ahead = from_behind(key_value2[:RIGHT], "tm", -1)
    joined = jnp.concatenate([key_value2, ahead], axis=0)
    cols2 = jnp.arange(fr + RIGHT, dtype=jnp.int32)
    spos2 = block * fr + cols2[None, :]
    allowed2 = (cols2[None, :] <= rows[:, None] + RIGHT) & ((spos2 < length) | (spos2 == tpos))
    ctx_two = attend(query2, joined[:, :width], joined[:, width:], allowed2, HEADS)
    valid = block * fr + rows < length
    context = jnp.where(valid[:, None], ctx_two, jnp.zeros_like(ctx_two))
    weight_grad = lax.psum_scatter(
        lax.dot_general(
            grad_in, context, (((0,), (0,)), ((), ())), preferred_element_type=jnp.float32
        ),
        ("tm", "fsdp"),
        scatter_dimension=0,
        tiled=True,
    )
    return (context[None], weight_grad)


MESH = pl.DeviceIdType.MESH


def flip(index, mask):
    out, bit = index, 1
    while bit <= mask:
        if mask & bit:
            out = out + bit * (1 - 2 * ((index // bit) % 2))
        bit *= 2
    return out


def heads_kernel(
    n,
    nz,
    frames_ref, gain_one_ref, qkv_one_ref, out_one_ref, gain_two_ref, qkv_two_ref,
    length_ref, count_ref, cot_ref,
    context_ref, grad_ref,
    nbuf, nbuf2, w1, w2, wo, cotv, cott, q1, k1, v1, ctx1s, ctx1, q2, k2, v2, ctx2s, ctx2,
    gsend, grecv, gsum, wgr,
    local_sem, ag_send, ag_recv, ch_send, ch_recv, a2_send, a2_recv, z_send, z_recv,
):
    t = lax.axis_index("tm")
    z = lax.axis_index("fsdp")
    fr, width = frames_ref.shape
    cols = width // n
    head = width // HEADS
    per = HEADS // n
    rows = width // nz
    part = rows // n
    scale = 1.0 / head**0.5
    mine = pl.multiple_of(t * cols, cols)

    def at_cols(index):
        return pl.ds(pl.multiple_of(index * cols, cols), cols)

    def at_rows(index, size):
        return pl.ds(pl.multiple_of(index * size, size), size)

    own_rows = at_rows(z, rows)
    local = []
    for j in range(3):
        for which, (src, dst) in enumerate(((qkv_one_ref, w1), (qkv_two_ref, w2))):
            local.append(
                pltpu.make_async_copy(
                    src.at[:, pl.ds(pl.multiple_of(j * width + mine, cols), cols)],
                    dst.at[own_rows, pl.ds(j * cols, cols)],
                    local_sem.at[2 * j + which],
                )
            )
    local.append(
        pltpu.make_async_copy(
            out_one_ref, wo.at[pl.ds(0, rows), :], local_sem.at[6]
        )
    )
    local.append(pltpu.make_async_copy(cot_ref, cotv, local_sem.at[7]))
    for copy in (local[6], local[0], local[2], local[4], local[7], local[1], local[3], local[5]):
        copy.start()

    barrier = pltpu.get_barrier_semaphore()
    for d in range(1, n):
        pl.semaphore_signal(
            barrier, inc=1, device_id=(lax.rem(t + d, n), z), device_id_type=MESH
        )
    for d in range(1, nz):
        pl.semaphore_signal(
            barrier, inc=1, device_id=(t, lax.rem(z + d, nz)), device_id_type=MESH
        )
    pl.semaphore_wait(barrier, n + nz - 2)

    half = rows // 2

    def chain_view(which, shard, h, at):
        place = lax.rem(shard - at + nz, nz) if which == 1 else shard
        span = pl.ds(pl.multiple_of(place * rows + h * half, half), half)
        if which == 1:
            return wo.at[span, pl.ds(mine, cols)]
        return (w1, None, w2)[which].at[span, :]

    def chain_copy(which, step, up, h):
        shard = z - step if up else z + step
        shard = jnp.clip(shard, 0, nz - 1)
        to = jnp.clip(z + 1 if up else z - 1, 0, nz - 1)
        return pltpu.make_async_remote_copy(
            src_ref=chain_view(which, shard, h, z),
            dst_ref=chain_view(which, shard, h, to),
            send_sem=ch_send.at[which, 0 if up else 1, step, h],
            recv_sem=ch_recv.at[which, shard, h],
            device_id=(t, to),
            device_id_type=MESH,
        )

    def chain_wait(which, shard, h, other):
        view = chain_view(which, shard, h, z)
        pltpu.make_async_remote_copy(
            src_ref=view,
            dst_ref=view,
            send_sem=ch_send.at[which, 0, 0, h],
            recv_sem=ch_recv.at[which, shard, h],
            device_id=(t, other),
            device_id_type=MESH,
        ).wait_recv()

    def chain_cond(step, up):
        if up:
            return (z >= step) & (z < nz - 1)
        return (z + step < nz) & (z > 0)

    def chain(which, step):
        for h in range(2):
            for up in (True, False):
                @pl.when(chain_cond(step, up))
                def _():
                    copy = chain_copy(which, step, up, h)
                    if step:
                        chain_wait(which, z - step if up else z + step, h, z + 1 if up else z - 1)
                    copy.start()

    def chain_end(which):
        for edge, up in ((nz - 1, True), (0, False)):
            @pl.when(z == edge)
            def _():
                for step in range(1, nz):
                    for h in range(2):
                        shard = edge - step if up else edge + step
                        chain_wait(which, shard, h, edge - 1 if up else edge + 1)

    def chain_sent(which):
        for step in range(nz - 1):
            for up in (True, False):
                for h in range(2):
                    @pl.when(chain_cond(step, up))
                    def _():
                        chain_copy(which, step, up, h).wait_send()

    def ag_view(which, index, piece):
        if which in (0, 3):
            buf = (nbuf, None, None, nbuf2)[which]
            if piece is None:
                return buf.at[index]
            return buf.at[index, pl.ds(piece * (fr // 2), fr // 2), :]
        buf, first = ((None, 0), (cott, 0), (wo, rows))[which]
        size = width - first
        if piece is None:
            return buf.at[pl.ds(first, size), at_cols(index)]
        return buf.at[pl.ds(first + piece * (size // 2), size // 2), at_cols(index)]

    slots = (
        (0, None, 1), (0, 0, 2), (0, 1, 2), (0, 1, 4), (0, 0, 4),
        (2, 0, 4), (4, 1, 2),
        (2, None, 1), (4, None, 1), (6, 0, 1), (6, 1, 1),
    )

    def ag_copy(which, slot):
        block, piece, to = slots[slot]
        view = ag_view(which, flip(t, block), piece)
        return pltpu.make_async_remote_copy(
            src_ref=view, dst_ref=view,
            send_sem=ag_send.at[which, slot], recv_sem=ag_recv.at[which, slot],
            device_id=(flip(t, to), z), device_id_type=MESH,
        )

    def ag_wait(which, slot):
        block, piece, to = slots[slot]
        view = ag_view(which, flip(t, block ^ to), piece)
        pltpu.make_async_remote_copy(
            src_ref=view, dst_ref=view,
            send_sem=ag_send.at[which, slot], recv_sem=ag_recv.at[which, slot],
            device_id=(flip(t, to), z), device_id_type=MESH,
        ).wait_recv()

    def ag_start(which):
        for slot in (1, 3, 2, 4, 0):
            ag_copy(which, slot).start()

    def ag_forward(which, stage):
        for waits, slot in (
            (((1, 5), (3, 6)), ((2, 7), (4, 8)), ((5, 9), (6, 10)))[stage]
        ):
            ag_wait(which, waits)
            ag_copy(which, slot).start()

    def ag_partner(which):
        for slot in (0, 7, 8, 9, 10):
            ag_wait(which, slot)

    def ag_sent(which):
        for slot in range(len(slots)):
            ag_copy(which, slot).wait_send()

    for j in (0, 2, 4):
        local[j].wait()
    chain(0, 0)
    local[6].wait()
    nbuf[t] = norm_rows(frames_ref[...], gain_one_ref[...])
    ag_start(0)
    local[7].wait()
    turned = cotv[...].T
    for zz in range(nz):
        for tt in range(n):
            cott[zz * rows + tt * part : zz * rows + (tt + 1) * part, pl.ds(mine, cols)] = turned[
                (tt * nz + zz) * part : (tt * nz + zz + 1) * part
            ]
    lead = LEFT_MAX * fr
    zeros = jnp.zeros((lead, cols), jnp.bfloat16)
    k1[0:lead, :] = zeros
    v1[0:lead, :] = zeros
    k2[n * fr :, :] = zeros[:fr]
    v2[n * fr :, :] = zeros[:fr]
    ag_forward(0, 0)
    chain(0, 1)
    chain(1, 0)
    ag_forward(0, 1)
    chain(0, 2)
    ag_forward(0, 2)
    ag_start(1)
    chain(1, 1)
    chain(1, 2)
    for j in (1, 3, 5):
        local[j].wait()
    chain(2, 0)

    def project(buf, weight, q, k, v, before, pair):
        left = buf[pl.ds(pair * 2, 2)].reshape(2 * fr, width)
        out = jnp.dot(left, weight[...], preferred_element_type=jnp.float32).astype(jnp.bfloat16)
        span = at_rows(pair, 2 * fr)
        q[span, :] = out[:, :cols]
        after = pl.ds(pl.multiple_of(pair * 2 * fr + before, fr), 2 * fr)
        k[after, :] = out[:, cols : 2 * cols]
        v[after, :] = out[:, 2 * cols :]

    ag_partner(0)
    chain_end(0)
    ag_forward(1, 0)
    for j in range(n // 2):
        project(nbuf, w1, q1, k1, v1, lead, j)
    chain_end(1)
    ag_start(2)
    ag_forward(1, 1)

    length = length_ref[0]
    count = count_ref[0]

    def attend_block(query, keys, values, allowed):
        lane = lax.broadcasted_iota(jnp.int32, (fr, cols), 1) // head
        blank = jnp.zeros_like(query)
        stacked = jnp.concatenate([jnp.where(lane == h, query, blank) for h in range(per)], axis=0)
        scores = lax.dot_general(
            stacked, keys, (((1,), (1,)), ((), ())), preferred_element_type=jnp.float32
        ) * scale
        scores = scores.reshape(per, fr, keys.shape[0])
        scores = jnp.where(allowed[None], scores, -1e30)
        top = jnp.max(scores, axis=-1, keepdims=True)
        expo = jnp.exp(scores - top)
        weights = expo * (1.0 / jnp.sum(expo, axis=-1, keepdims=True))
        weights = weights.astype(jnp.bfloat16).reshape(per * fr, keys.shape[0])
        mixed = jnp.dot(weights, values, preferred_element_type=jnp.float32)
        out = mixed[:fr]
        for h in range(1, per):
            out = jnp.where(lane == h, mixed[h * fr : (h + 1) * fr], out)
        return out.astype(jnp.bfloat16)

    def causal(b):
        span = pl.ds(pl.multiple_of(b * fr, fr), lead + fr)
        shape = (fr, lead + fr)
        row = lax.broadcasted_iota(jnp.int32, shape, 0)
        col = lax.broadcasted_iota(jnp.int32, shape, 1)
        spos = (b - LEFT_MAX) * fr + col
        tpos = b * fr + row
        apart = LEFT_MAX - col // fr
        allowed = (spos >= 0) & (spos <= tpos) & (apart <= count)
        allowed = allowed & ((spos < length) | (spos == tpos))
        return attend_block(q1[at_rows(b, fr), :], k1[span, :], v1[span, :], allowed)

    def ahead(b):
        span = pl.ds(pl.multiple_of(b * fr, fr), 2 * fr)
        shape = (fr, 2 * fr)
        row = lax.broadcasted_iota(jnp.int32, shape, 0)
        col = lax.broadcasted_iota(jnp.int32, shape, 1)
        spos = b * fr + col
        allowed = (col <= row + RIGHT) & ((spos < length) | (col == row))
        out = attend_block(q2[at_rows(b, fr), :], k2[span, :], v2[span, :], allowed)
        valid = b * fr + lax.broadcasted_iota(jnp.int32, (fr, cols), 0) < length
        return jnp.where(valid, out, jnp.zeros_like(out))

    def turned_cols(which, index):
        return lax.rem(index - z * (rows // cols) + n, n) if which == 0 else index

    def back_copy(which, d):
        src, dst = ((ctx1s, ctx1), (ctx2s, ctx2))[which]
        b = lax.rem(t + d, n)
        return pltpu.make_async_remote_copy(
            src_ref=src.at[at_rows(b, fr), :],
            dst_ref=dst.at[:, at_cols(turned_cols(which, t))],
            send_sem=a2_send.at[which, d], recv_sem=a2_recv.at[which, d],
            device_id=(b, z), device_id_type=MESH,
        )

    def back_wait(which):
        src, dst = ((ctx1s, ctx1), (ctx2s, ctx2))[which]
        for d in range(1, n):
            b = lax.rem(t + n - d, n)
            pltpu.make_async_remote_copy(
                src_ref=src.at[at_rows(b, fr), :],
                dst_ref=dst.at[:, at_cols(turned_cols(which, b))],
                send_sem=a2_send.at[which, d], recv_sem=a2_recv.at[which, d],
                device_id=(b, z), device_id_type=MESH,
            ).wait_recv()

    def blocks(which, first, last):
        fun, src = ((causal, ctx1s), (ahead, ctx2s))[which]

        def body(d, carry):
            b = lax.rem(t + d, n)
            src[at_rows(b, fr), :] = fun(b)
            back_copy(which, d).start()
            return carry

        lax.fori_loop(first, last, body, 0)

    def own_block(which):
        fun, src, dst = ((causal, ctx1s, ctx1), (ahead, ctx2s, ctx2))[which]
        out = fun(t)
        src[at_rows(t, fr), :] = out
        dst[:, at_cols(turned_cols(which, t))] = out

    blocks(0, 1, n // 2)
    ag_forward(1, 2)
    chain(2, 1)
    blocks(0, n // 2, n)
    own_block(0)
    ag_forward(2, 0)
    ag_forward(2, 1)
    ag_forward(2, 2)
    ag_partner(2)
    back_wait(0)

    mixed = jnp.dot(ctx1[...], wo[...], preferred_element_type=jnp.float32)
    hidden = (frames_ref[...].astype(jnp.float32) + mixed).astype(jnp.bfloat16)
    nbuf2[t] = norm_rows(hidden, gain_two_ref[...])
    ag_start(3)
    for step in range(2, nz - 1):
        chain(2, step)
    ag_forward(3, 0)
    chain_end(2)
    ag_wait(3, 0)
    project(nbuf2, w2, q2, k2, v2, 0, t // 2)
    ag_forward(3, 1)
    ag_wait(3, 7)
    project(nbuf2, w2, q2, k2, v2, 0, flip(t, 2) // 2)
    ag_wait(3, 8)
    project(nbuf2, w2, q2, k2, v2, 0, flip(t, 4) // 2)
    ag_forward(3, 2)
    ag_wait(3, 9)
    ag_wait(3, 10)
    project(nbuf2, w2, q2, k2, v2, 0, flip(t, 6) // 2)
    blocks(1, 1, n)
    own_block(1)
    ag_partner(1)

    def term(zz):
        return jnp.dot(
            cott[at_rows(zz, rows), :], ctx2s[...], preferred_element_type=jnp.float32
        )

    def z_copy(d, back):
        to = lax.rem(z + d, nz)
        return pltpu.make_async_remote_copy(
            src_ref=gsend.at[d], dst_ref=grecv.at[d],
            send_sem=z_send.at[d], recv_sem=z_recv.at[d],
            device_id=(t, to), device_id_type=MESH,
        )

    for d in range(1, nz):
        gsend[d] = term(lax.rem(z + d, nz)).astype(jnp.bfloat16)
        z_copy(d, False).start()
    total = term(z)
    for d in range(1, nz):
        z_copy(d, True).wait_recv()
        total = total + grecv[d].astype(jnp.float32)
    gsum[...] = total

    def g_copy(d):
        b = lax.rem(t + d, n)
        return pltpu.make_async_remote_copy(
            src_ref=gsum.at[at_rows(b, part), :],
            dst_ref=wgr.at[:, pl.ds(mine, cols)],
            send_sem=a2_send.at[2, d], recv_sem=a2_recv.at[2, d],
            device_id=(b, z), device_id_type=MESH,
        )

    for d in range(1, n):
        g_copy(d).start()
    wgr[:, pl.ds(mine, cols)] = gsum[at_rows(t, part), :]
    back_wait(1)
    context_ref[...] = ctx2[...]
    for d in range(1, n):
        b = lax.rem(t + n - d, n)
        pltpu.make_async_remote_copy(
            src_ref=gsum.at[at_rows(b, part), :],
            dst_ref=wgr.at[:, at_cols(b)],
            send_sem=a2_send.at[2, d], recv_sem=a2_recv.at[2, d],
            device_id=(b, z), device_id_type=MESH,
        ).wait_recv()
    grad_ref[...] = wgr[...]
    for which in range(4):
        ag_sent(which)
    for which in range(3):
        chain_sent(which)
    for d in range(1, n):
        back_copy(0, d).wait_send()
        back_copy(1, d).wait_send()
        g_copy(d).wait_send()
    for d in range(1, nz):
        z_copy(d, False).wait_send()


def hand_out(context_ref, grad_ref, context_out, grad_out):
    context_out[...] = context_ref[...]
    grad_out[...] = grad_ref[...]


def by_heads(
    n, nz, frames, gain_one, qkv_one, out_one, gain_two, qkv_two, lengths, left_counts, cotangent
):
    _, fr, width = frames.shape
    cols = width // n
    rows = width // nz
    span = n * fr
    vmem = pl.BlockSpec(memory_space=pltpu.VMEM)
    smem = pl.BlockSpec(memory_space=pltpu.SMEM)
    hbm = pl.BlockSpec(memory_space=pl.ANY)
    bf16, f32 = jnp.bfloat16, jnp.float32
    dma = pltpu.SemaphoreType.DMA
    context, grad = pl.pallas_call(
        functools.partial(heads_kernel, n, nz),
        out_shape=(
            jax.ShapeDtypeStruct((fr, width), bf16),
            jax.ShapeDtypeStruct((rows // n, width), f32),
        ),
        in_specs=[vmem, vmem, hbm, hbm, vmem, hbm, smem, smem, hbm],
        out_specs=(vmem, vmem),
        scratch_shapes=[
            pltpu.VMEM((n, fr, width), bf16),
            pltpu.VMEM((n, fr, width), bf16),
            pltpu.VMEM((width, 3 * cols), bf16),
            pltpu.VMEM((width, 3 * cols), bf16),
            pltpu.VMEM((width, width), bf16),
            pltpu.VMEM((fr, width), bf16),
            pltpu.VMEM((width, span), bf16),
            pltpu.VMEM((span, cols), bf16),
            pltpu.VMEM((span + LEFT_MAX * fr, cols), bf16),
            pltpu.VMEM((span + LEFT_MAX * fr, cols), bf16),
            pltpu.VMEM((span, cols), bf16),
            pltpu.VMEM((fr, width), bf16),
            pltpu.VMEM((span, cols), bf16),
            pltpu.VMEM((span + fr, cols), bf16),
            pltpu.VMEM((span + fr, cols), bf16),
            pltpu.VMEM((span, cols), bf16),
            pltpu.VMEM((fr, width), bf16),
            pltpu.VMEM((nz, rows, cols), bf16),
            pltpu.VMEM((nz, rows, cols), bf16),
            pltpu.VMEM((rows, cols), f32),
            pltpu.VMEM((rows // n, width), f32),
            dma((8,)),
            dma((4, 11)),
            dma((4, 11)),
            dma((3, 2, nz, 2)),
            dma((3, nz, 2)),
            dma((3, n)),
            dma((3, n)),
            dma((nz,)),
            dma((nz,)),
        ],
        compiler_params=pltpu.CompilerParams(
            collective_id=0, has_side_effects=True, vmem_limit_bytes=60 * 1024 * 1024
        ),
    )(
        frames[0], gain_one[None], qkv_one, out_one, gain_two[None], qkv_two,
        lengths, left_counts, cotangent[0],
    )
    context, grad = pl.pallas_call(
        hand_out,
        out_shape=(
            jax.ShapeDtypeStruct((fr, width), bf16),
            jax.ShapeDtypeStruct((rows // n, width), f32),
        ),
        in_specs=[vmem, vmem],
        out_specs=(vmem, vmem),
    )(context, grad)
    return (context[None], grad)


def solution(mesh):
    n_tm = mesh.shape["tm"]
    even = n_tm == 2 * CHIPS and mesh.shape["fsdp"] == CHIPS and HEADS % n_tm == 0
    chosen = functools.partial(by_heads, n_tm, mesh.shape["fsdp"]) if even else on_device
    in_specs = (
        P("fsdp", "tm", None),
        P(),
        P("fsdp", None),
        P("fsdp", None),
        P(),
        P("fsdp", None),
        P("fsdp"),
        P("fsdp"),
        P("fsdp", "tm", None),
    )
    out_specs = (P("fsdp", "tm", None), P(("tm", "fsdp"), None))
    return jax.shard_map(
        chosen, mesh=mesh, in_specs=in_specs, out_specs=out_specs, check_vma=False
    )
```

profile of v0, /device:TPU:0, one launch (start us, length us, event | category | flops | bytes accessed | tf_op | source)
XLA Modules:
  0.0 70.5 jit_solution(7808191045961995028)
XLA Ops:
  1.9 66.8 %shard_map.104 = (bf16[128,1024]{1,0:T(8,128)(2,1)}, f32[32,1024]{1,0:T(8,128)}) custom-call(bf16[128,1024]{1,0:T(8,128)(2,1)} %bitcast.5, f32[1,1024]{1,0:T(1,128)} %bitcast.7, bf16[256,3072]{1,0:T(8,128)(2,1)} %qkv_one_ref.1, bf16[256,1024]{1,0:T(8,128)(2,1)} %out_one_ref.1, f32[1,1024]{1,0:T(1,128)} %bitcast.8, bf16[256,3072]{1,0:T(8,128)(2,1)} %qkv_two_ref.1, ...), custom_call_target="tpu_custom_call" | custom-call | tf_op jit(solution)/shard_map/pallas_call | solution.py:534
  68.7 1.7 %shard_map.105 = (bf16[128,1024]{1,0:T(8,128)(2,1)}, f32[32,1024]{1,0:T(8,128)}) custom-call(bf16[128,1024]{1,0:T(8,128)(2,1)} %get-tuple-element.6.context_ref, f32[32,1024]{1,0:T(8,128)} %get-tuple-element.7.grad_ref), custom_call_target="tpu_custom_call" | custom-call | tf_op jit(solution)/shard_map/pallas_call | solution.py:581
where the time goes:
time: 70.6 us; the launch traced here: 70.5 us
  Pallas kernels  68.5 us (97%)
  between operations  1.93 us (3%)
    pallas_call x1, Pallas kernels, by_heads(): pl.pallas_call(functools.partial(heads_kernel, n, nz), out_shape=(jax.Sha...  66.8 us
    pallas_call x1, Pallas kernels, by_heads(): pl.pallas_call(hand_out, out_shape=(jax.ShapeDtypeStruct((fr, width), bf1...  1.74 us

commit v1 on v0

v1 whole, which is shorter than its diff:
```python
import contextlib
import functools
import math

import jax
import jax.numpy as jnp
from jax import lax
from jax.experimental import pallas as pl
from jax.experimental.pallas import tpu as pltpu
from jax.sharding import PartitionSpec as P

HEADS = 16
LEFT_MAX = 2
RIGHT = 23
CHIPS = 4
SCOPES = False


def mark(name):
    return jax.named_scope(name) if SCOPES else contextlib.nullcontext()


def from_behind(block, axis, distance):
    devices = range(lax.axis_size(axis))
    route = [(i - distance, i) for i in devices if i - distance in devices]
    return lax.ppermute(block, axis, route)


def norm_rows(values, gain):
    wide = values.astype(jnp.float32)
    mean = jnp.mean(wide, axis=-1, keepdims=True)
    var = jnp.mean((wide - mean) ** 2, axis=-1, keepdims=True)
    return ((wide - mean) * lax.rsqrt(var + 1e-05) * gain).astype(jnp.bfloat16)


def attend(query, keys, values, allowed, heads):
    rows_q, width = query.shape
    head = width // heads
    scale = 1.0 / head**0.5
    q_heads = query.reshape(rows_q, heads, head)
    k_heads = keys.reshape(keys.shape[0], heads, head)
    v_heads = values.reshape(values.shape[0], heads, head)
    scores = (
        jnp.einsum("qhe,khe->hqk", q_heads, k_heads, preferred_element_type=jnp.float32) * scale
    )
    scores = jnp.where(allowed[None], scores, -1e30)
    top = jnp.max(scores, axis=-1, keepdims=True)
    expo = jnp.exp(scores - top)
    weights = (expo / jnp.sum(expo, axis=-1, keepdims=True)).astype(jnp.bfloat16)
    ctx = jnp.einsum("hqk,khe->qhe", weights, v_heads, preferred_element_type=jnp.float32)
    return ctx.reshape(rows_q, width).astype(jnp.bfloat16)


def add_rows(left, piece):
    return jnp.dot(left, piece, preferred_element_type=jnp.float32)


def on_device(
    frames, gain_one, qkv_one, out_one, gain_two, qkv_two, lengths, left_counts, cotangent
):
    local = frames[0]
    grad_in = cotangent[0]
    fr, width = local.shape
    block = lax.axis_index("tm")
    length = lengths[0]
    count = left_counts[0]
    norm_one = norm_rows(local, gain_one)
    proj = add_rows(norm_one, lax.all_gather(qkv_one, "fsdp", axis=0, tiled=True))
    proj = proj.astype(jnp.bfloat16)
    query = proj[:, :width]
    key_value = proj[:, width:]
    earlier = [from_behind(key_value, "tm", step) for step in range(LEFT_MAX, 0, -1)]
    gathered = jnp.concatenate(earlier + [key_value], axis=0)
    rows = jnp.arange(fr, dtype=jnp.int32)
    cols = jnp.arange((LEFT_MAX + 1) * fr, dtype=jnp.int32)
    tpos = block * fr + rows[:, None]
    spos = (block - LEFT_MAX) * fr + cols[None, :]
    apart = LEFT_MAX - cols[None, :] // fr
    allowed = (spos >= 0) & (spos <= tpos) & (apart <= count) & ((spos < length) | (spos == tpos))
    ctx_one = attend(query, gathered[:, :width], gathered[:, width:], allowed, HEADS)
    out_proj = add_rows(ctx_one, lax.all_gather(out_one, "fsdp", axis=0, tiled=True))
    hidden = (local.astype(jnp.float32) + out_proj).astype(jnp.bfloat16)
    norm_two = norm_rows(hidden, gain_two)
    proj2 = add_rows(norm_two, lax.all_gather(qkv_two, "fsdp", axis=0, tiled=True))
    proj2 = proj2.astype(jnp.bfloat16)
    query2 = proj2[:, :width]
    key_value2 = proj2[:, width:]
    ahead = from_behind(key_value2[:RIGHT], "tm", -1)
    joined = jnp.concatenate([key_value2, ahead], axis=0)
    cols2 = jnp.arange(fr + RIGHT, dtype=jnp.int32)
    spos2 = block * fr + cols2[None, :]
    allowed2 = (cols2[None, :] <= rows[:, None] + RIGHT) & ((spos2 < length) | (spos2 == tpos))
    ctx_two = attend(query2, joined[:, :width], joined[:, width:], allowed2, HEADS)
    valid = block * fr + rows < length
    context = jnp.where(valid[:, None], ctx_two, jnp.zeros_like(ctx_two))
    weight_grad = lax.psum_scatter(
        lax.dot_general(
            grad_in, context, (((0,), (0,)), ((), ())), preferred_element_type=jnp.float32
        ),
        ("tm", "fsdp"),
        scatter_dimension=0,
        tiled=True,
    )
    return (context[None], weight_grad)


MESH = pl.DeviceIdType.MESH


def flip(index, mask):
    out, bit = index, 1
    while bit <= mask:
        if mask & bit:
            out = out + bit * (1 - 2 * ((index // bit) % 2))
        bit *= 2
    return out


def heads_kernel(
    n,
    nz,
    frames_ref, gain_one_ref, qkv_one_ref, out_one_ref, gain_two_ref, qkv_two_ref,
    length_ref, count_ref, cot_ref,
    context_ref, grad_ref,
    fbuf, nbuf, nbuf2, w1, w2, wo, cotv, cott, gains,
    q1, k1a, k1b, v1a, v1b, p1, r1, ctx1s, ctxall,
    q2, k2a, k2b, v2a, v2b, p2, pn2, r2, ctx2s, ctx2,
    gsend, grecv, gsum, wgr,
    local_sem, ag_send, ag_recv, ch_send, ch_recv, cx_send, cx_recv, nx_send, nx_recv,
    a2_send, a2_recv, z_send, z_recv,
):
    t = lax.axis_index("tm")
    z = lax.axis_index("fsdp")
    fr, width = frames_ref.shape
    cols = width // n
    head = width // HEADS
    per = HEADS // n
    rows = width // nz
    part = rows // n
    groups = n // 2
    scale = math.log2(math.e) / head**0.5
    mine = pl.multiple_of(t * cols, cols)
    core = lax.rem(t, 2)

    def at_cols(index):
        return pl.ds(pl.multiple_of(index * cols, cols), cols)

    def at_rows(index, size):
        return pl.ds(pl.multiple_of(index * size, size), size)

    barrier = pltpu.get_barrier_semaphore()
    for mask in (4, 2, 1):
        pl.semaphore_signal(barrier, inc=1, device_id=(flip(t, mask), z), device_id_type=MESH)

    @pl.when(z > 0)
    def _():
        pl.semaphore_signal(barrier, inc=1, device_id=(t, z - 1), device_id_type=MESH)

    @pl.when(z < nz - 1)
    def _():
        pl.semaphore_signal(barrier, inc=1, device_id=(t, z + 1), device_id_type=MESH)

    own_rows = at_rows(z, rows)

    def load(src, dst, index):
        return pltpu.make_async_copy(src, dst, local_sem.at[index])

    def load_cols(src, dst, j, index):
        return load(
            src.at[:, pl.ds(pl.multiple_of(j * width + mine, cols), cols)],
            dst.at[own_rows, pl.ds(j * cols, cols)],
            index,
        )

    get_frames = load(frames_ref, fbuf.at[t], 0)
    get_wo = load(out_one_ref, wo.at[pl.ds(0, rows), :], 1)
    get_w1 = [load_cols(qkv_one_ref, w1, j, 2 + j) for j in range(3)]
    get_w2 = [load_cols(qkv_two_ref, w2, j, 5 + j) for j in range(3)]
    get_cot = load(cot_ref, cotv, 8)
    get_gains = [load(gain_one_ref, gains.at[0:1], 9), load(gain_two_ref, gains.at[1:2], 10)]
    for copy in [get_frames, get_wo, *get_w1, *get_gains, get_cot, *get_w2]:
        copy.start()

    half = rows // 2

    def chain_view(which, shard, h, at):
        place = lax.rem(shard - at + nz, nz) if which == 0 else shard
        span = pl.ds(pl.multiple_of(place * rows + h * half, half), half)
        if which == 0:
            return wo.at[span, pl.ds(mine, cols)]
        wide = pl.ds(0, 2 * cols) if which in (1, 3) else pl.ds(2 * cols, cols)
        return (w1 if which < 3 else w2).at[span, wide]

    def chain_copy(which, step, up, h):
        shard = z - step if up else z + step
        shard = jnp.clip(shard, 0, nz - 1)
        to = jnp.clip(z + 1 if up else z - 1, 0, nz - 1)
        return pltpu.make_async_remote_copy(
            src_ref=chain_view(which, shard, h, z),
            dst_ref=chain_view(which, shard, h, to),
            send_sem=ch_send.at[which, 0 if up else 1, step, h],
            recv_sem=ch_recv.at[which, shard, h],
            device_id=(t, to),
            device_id_type=MESH,
        )

    def chain_wait(which, shard, h, other):
        view = chain_view(which, shard, h, z)
        pltpu.make_async_remote_copy(
            src_ref=view,
            dst_ref=view,
            send_sem=ch_send.at[which, 0, 0, h],
            recv_sem=ch_recv.at[which, shard, h],
            device_id=(t, other),
            device_id_type=MESH,
        ).wait_recv()

    def chain_cond(step, up):
        if up:
            return (z >= step) & (z < nz - 1)
        return (z + step < nz) & (z > 0)

    def chain(which, step, halves=(0, 1)):
        for h in halves:
            for up in (True, False):
                @pl.when(chain_cond(step, up))
                def _():
                    copy = chain_copy(which, step, up, h)
                    if step:
                        chain_wait(which, z - step if up else z + step, h, z + 1 if up else z - 1)
                    copy.start()

    def chain_end(which):
        for edge, up in ((nz - 1, True), (0, False)):
            @pl.when(z == edge)
            def _():
                for step in range(1, nz):
                    for h in range(2):
                        shard = edge - step if up else edge + step
                        chain_wait(which, shard, h, edge - 1 if up else edge + 1)

    def chain_sent(which):
        for step in range(nz - 1):
            for up in (True, False):
                for h in range(2):
                    @pl.when(chain_cond(step, up))
                    def _():
                        chain_copy(which, step, up, h).wait_send()

    def ag_view(which, index, piece):
        if which == 0:
            if piece is None:
                return fbuf.at[index]
            return fbuf.at[index, pl.ds(piece * (fr // 2), fr // 2), :]
        buf, first, size = (
            None, (cott, 0, width // 2), (wo, rows, width - rows), (cott, width // 2, width // 2),
        )[which]
        if piece is None:
            return buf.at[pl.ds(first, size), at_cols(index)]
        return buf.at[pl.ds(first + piece * (size // 2), size // 2), at_cols(index)]

    slots = (
        (0, None, 1), (0, 0, 2), (0, 1, 2), (0, 1, 4), (0, 0, 4),
        (2, 0, 4), (4, 1, 2),
        (2, None, 1), (4, None, 1), (6, 0, 1), (6, 1, 1),
    )

    def ag_copy(which, slot):
        block, piece, to = slots[slot]
        view = ag_view(which, flip(t, block), piece)
        return pltpu.make_async_remote_copy(
            src_ref=view, dst_ref=view,
            send_sem=ag_send.at[which, slot], recv_sem=ag_recv.at[which, slot],
            device_id=(flip(t, to), z), device_id_type=MESH,
        )

    def ag_wait(which, slot):
        block, piece, to = slots[slot]
        view = ag_view(which, flip(t, block ^ to), piece)
        pltpu.make_async_remote_copy(
            src_ref=view, dst_ref=view,
            send_sem=ag_send.at[which, slot], recv_sem=ag_recv.at[which, slot],
            device_id=(flip(t, to), z), device_id_type=MESH,
        ).wait_recv()

    def ag_start(which):
        for slot in (1, 3, 2, 4, 0):
            ag_copy(which, slot).start()

    def ag_forward(which, stage):
        for waits, slot in (
            (((1, 5), (3, 6)), ((2, 7), (4, 8)), ((5, 9), (6, 10)))[stage]
        ):
            ag_wait(which, waits)
            ag_copy(which, slot).start()

    def ag_partner(which):
        for slot in (0, 7, 8, 9, 10):
            ag_wait(which, slot)

    def ag_sent(which):
        for slot in range(len(slots)):
            ag_copy(which, slot).wait_send()

    def normed(index):
        nbuf[index] = norm_rows(fbuf[index], gains[0:1, :])

    def masked_heads(values):
        lane = lax.broadcasted_iota(jnp.int32, values.shape, 1) // head
        blank = jnp.zeros_like(values)
        return jnp.where(lane == 0, values, blank), jnp.where(lane == 1, values, blank)

    def dot(left, right):
        return jnp.dot(left, right, preferred_element_type=jnp.float32)

    def dot_t(left, right):
        return lax.dot_general(
            left, right, (((1,), (1,)), ((), ())), preferred_element_type=jnp.float32
        )

    def project(buf, weight, pair, targets_qk, targets_v):
        left = buf[2 * pair : 2 * pair + 2].reshape(2 * fr, width)
        span = pl.ds(2 * pair * fr, 2 * fr)
        if targets_qk is not None:
            q, ka, kb = targets_qk
            out = dot(left, weight[:, : 2 * cols]).astype(jnp.bfloat16)
            q[span, :] = out[:, :cols]
            ka[span, :], kb[span, :] = masked_heads(out[:, cols:])
        else:
            va, vb = targets_v
            out = dot(left, weight[:, 2 * cols :]).astype(jnp.bfloat16)
            va[span, :], vb[span, :] = masked_heads(out)

    def turned(index):
        return lax.rem(index - z * (rows // cols) + n, n)

    with mark("a_barrier"):
        pl.semaphore_wait(
            barrier, 3 + jnp.where(z > 0, 1, 0) + jnp.where(z < nz - 1, 1, 0)
        )
    with mark("b_frames"):
        get_frames.wait()
    ag_start(0)
    get_wo.wait()
    chain(0, 0)
    with mark("c_w1local"):
        get_w1[0].wait()
        get_w1[1].wait()
    chain(1, 0, (0,))
    with mark("d_norm"):
        for copy in get_gains:
            copy.wait()
        normed(t)
    with mark("e_chain01"):
        chain(0, 1)
    chain(1, 0, (1,))
    with mark("f_agf00"):
        ag_forward(0, 0)
    with mark("g_turn"):
        get_cot.wait()
        turned_cot = cotv[...].T
        for zz in range(nz):
            for tt in range(n):
                cott[zz * rows + tt * part : zz * rows + (tt + 1) * part, pl.ds(mine, cols)] = (
                    turned_cot[(tt * nz + zz) * part : (tt * nz + zz + 1) * part]
                )
        ag_wait(0, 0)
        normed(flip(t, 1))
    with mark("h_chain02"):
        chain(0, 2)
    with mark("i_agf01"):
        ag_forward(0, 1)
    with mark("j_chain11"):
        chain(1, 1)
    with mark("k_chainend0"):
        chain_end(0)
    ag_start(2)
    with mark("l_norms"):
        normed(flip(t, 2))
        normed(flip(t, 4))
    with mark("m_chain12"):
        chain(1, 2)
    get_w1[2].wait()
    chain(2, 0)
    with mark("n_agf02"):
        ag_forward(0, 2)
    with mark("o_norms"):
        ag_wait(0, 7)
        normed(flip(t, 3))
        ag_wait(0, 8)
        normed(flip(t, 5))
        normed(flip(t, 6))
    with mark("p_agf20"):
        ag_forward(2, 0)
    with mark("q_norm"):
        ag_wait(0, 9)
        ag_wait(0, 10)
        normed(flip(t, 7))
    with mark("r_chainend1"):
        chain_end(1)
    with mark("s_projqk"):
        for pair in range(groups):
            project(nbuf, w1, pair, (q1, k1a, k1b), None)

    length = length_ref[0]
    count = count_ref[0]
    row = lax.broadcasted_iota(jnp.int32, (fr, fr), 0)
    col = lax.broadcasted_iota(jnp.int32, (fr, fr), 1)
    low = -1e30

    def spans(b):
        first = max(b - LEFT_MAX, 0)
        return pl.ds(first * fr, (b + 1 - first) * fr), b - first

    def causal(b):
        span, before = spans(b)
        size = (before + 1) * fr
        query = q1[b * fr : (b + 1) * fr, :]
        both = dot_t(query, jnp.concatenate([k1a[span, :], k1b[span, :]], axis=0))
        spos = (b - before) * fr + lax.broadcasted_iota(jnp.int32, (1, size), 1)
        apart = before - lax.broadcasted_iota(jnp.int32, (1, size), 1) // fr
        bias = jnp.where((apart <= count) & (spos < length), 0.0, low)
        expos, inverse = [], []
        for h in range(per):
            scores = both[:, h * size : (h + 1) * size]
            now = scores[:, before * fr :]
            now = jnp.where(
                row > col,
                now + bias[:, before * fr :],
                jnp.where(row == col, now, low),
            )
            if before:
                now = jnp.concatenate(
                    [scores[:, : before * fr] + bias[:, : before * fr], now], axis=1
                )
            top = jnp.max(now, axis=-1, keepdims=True)
            expo = jnp.exp2((now - top) * scale)
            inverse.append(1.0 / jnp.sum(expo, axis=-1, keepdims=True))
            expos.append(expo.astype(jnp.bfloat16))
        p1[b, :, : per * size] = jnp.concatenate(expos, axis=1)
        r1[b] = jnp.where(col // head == 0, inverse[0], inverse[1])

    def causal_mix(b):
        span, before = spans(b)
        size = (before + 1) * fr
        mixed = dot(
            p1[b, :, : per * size], jnp.concatenate([v1a[span, :], v1b[span, :]], axis=0)
        )
        ctx1s[b * fr : (b + 1) * fr, :] = (mixed * r1[b]).astype(jnp.bfloat16)

    with mark("t_soft0"):
        causal(0)
        causal(1)
    with mark("ta_chain21"):
        chain(2, 1)
    with mark("tb_agf21"):
        ag_forward(2, 1)
    with mark("t_soft1"):
        causal(2)
        causal(3)
    with mark("tc_chain22"):
        chain(2, 2, (0,))
    with mark("td_agf22"):
        ag_forward(2, 2)
    ag_start(1)
    with mark("t_soft2"):
        causal(4)
        causal(5)
    with mark("te_chain22"):
        chain(2, 2, (1,))
    for copy in get_w2:
        copy.wait()
    chain(3, 0)
    with mark("t_soft3"):
        causal(6)
        causal(7)
    with mark("u_agf10"):
        ag_forward(1, 0)
    with mark("v_chainend2"):
        chain_end(2)
    with mark("w_projv"):
        for pair in range(groups):
            project(nbuf, w1, pair, None, (v1a, v1b))

    def cx_copy(g, m):
        to = flip(t, (m, 4, 2)[max(m - 5, 0)])
        if m < 6:
            src = ctx1s.at[at_rows(2 * g + lax.rem(core + m, 2), fr), :]
            dst = ctxall.at[g, :, at_cols(turned(t))]
        else:
            first = turned(flip(t, 2 if m == 6 else 4) // 2 * 2)
            src = ctxall.at[
                g,
                pl.ds((m - 6) * (fr // 2), fr // 2),
                pl.ds(pl.multiple_of(first * cols, 2 * cols), 2 * cols),
            ]
            dst = src
        return pltpu.make_async_remote_copy(
            src_ref=src, dst_ref=dst,
            send_sem=cx_send.at[g, m], recv_sem=cx_recv.at[g, m],
            device_id=(to, z), device_id_type=MESH,
        )

    def cx_wait(g, m):
        to = flip(t, (m, 4, 2)[max(m - 5, 0)])
        if m < 6:
            view = ctxall.at[g, :, at_cols(turned(to))]
        else:
            view = ctxall.at[
                g,
                pl.ds((m - 6) * (fr // 2), fr // 2),
                pl.ds(pl.multiple_of(turned(flip(t, 6) // 2 * 2) * cols, 2 * cols), 2 * cols),
            ]
        pltpu.make_async_remote_copy(
            src_ref=view, dst_ref=view,
            send_sem=cx_send.at[g, m], recv_sem=cx_recv.at[g, m],
            device_id=(to, z), device_id_type=MESH,
        ).wait_recv()

    def cx_forward(g):
        cx_wait(g, 2)
        cx_wait(g, 3)
        cx_copy(g, 6).start()
        cx_wait(g, 4)
        cx_wait(g, 5)
        cx_copy(g, 7).start()

    with mark("x_mix"):
        for g in range(groups):
            causal_mix(2 * g)
            causal_mix(2 * g + 1)
            for m in (2, 4, 3, 5, 1):
                cx_copy(g, m).start()
            ctxall[g, :, at_cols(turned(t))] = ctx1s[at_rows(2 * g + core, fr), :]
    with mark("xa_agf11"):
        ag_forward(1, 1)
    with mark("xb_chain31"):
        chain(3, 1)
    with mark("xc_agf12"):
        ag_forward(1, 2)
    with mark("xd_fwd0"):
        cx_forward(0)
    with mark("xe_agp2"):
        ag_partner(2)
    with mark("xf_fwd1"):
        cx_forward(1)
    with mark("xg_chain32"):
        chain(3, 2)
    chain(4, 0)
    with mark("xh_fwd2"):
        cx_forward(2)
    with mark("xi_fwd3"):
        cx_forward(3)
    ag_start(3)
    with mark("xj_agp1"):
        ag_partner(1)

    def nx_copy(g, other):
        view = nbuf2.at[2 * g + (1 - core if other else core)]
        return pltpu.make_async_remote_copy(
            src_ref=view, dst_ref=view,
            send_sem=nx_send.at[g], recv_sem=nx_recv.at[g],
            device_id=(flip(t, 1), z), device_id_type=MESH,
        )

    def out_block(g):
        for m in (1, 6, 7):
            cx_wait(g, m)
        b = 2 * g + core
        mixed = dot(ctxall[g], wo[...])
        hidden = (fbuf[b].astype(jnp.float32) + mixed).astype(jnp.bfloat16)
        nbuf2[b] = norm_rows(hidden, gains[1:2, :])
        nx_copy(g, False).start()

    tail = -(-RIGHT // 16) * 16
    wide = lax.broadcasted_iota(jnp.int32, (tail, tail), 1)
    long = lax.broadcasted_iota(jnp.int32, (tail, tail), 0) + (fr - tail)

    def ahead(b):
        query = q2[b * fr : (b + 1) * fr, :]
        here = pl.ds(b * fr, fr)
        both = dot_t(query, jnp.concatenate([k2a[here, :], k2b[here, :]], axis=0))
        seen = jnp.where(b * fr + lax.broadcasted_iota(jnp.int32, (1, fr), 1) < length, 0.0, low)
        after = None
        if b < n - 1:
            there = pl.ds((b + 1) * fr, tail)
            after = dot_t(
                query[fr - tail :], jnp.concatenate([k2a[there, :], k2b[there, :]], axis=0)
            )
            spos = (b + 1) * fr + lax.broadcasted_iota(jnp.int32, (1, tail), 1)
            late = jnp.where(spos < length, 0.0, low)
        expos, lates, inverse = [], [], []
        for h in range(per):
            now = both[:, h * fr : (h + 1) * fr]
            now = jnp.where(
                row == col, now, jnp.where(col <= row + RIGHT, now + seen, low)
            )
            top = jnp.max(now, axis=-1, keepdims=True)
            if after is not None:
                then = after[:, h * tail : (h + 1) * tail]
                then = jnp.where(wide + fr <= long + RIGHT, then + late, low)
                top = jnp.concatenate(
                    [
                        top[: fr - tail],
                        jnp.maximum(top[fr - tail :], jnp.max(then, axis=-1, keepdims=True)),
                    ],
                    axis=0,
                )
            expo = jnp.exp2((now - top) * scale)
            total = jnp.sum(expo, axis=-1, keepdims=True)
            if after is not None:
                then = jnp.exp2((then - top[fr - tail :]) * scale)
                total = jnp.concatenate(
                    [
                        total[: fr - tail],
                        total[fr - tail :] + jnp.sum(then, axis=-1, keepdims=True),
                    ],
                    axis=0,
                )
                lates.append(then.astype(jnp.bfloat16))
            inverse.append(1.0 / total)
            expos.append(expo.astype(jnp.bfloat16))
        p2[b] = jnp.concatenate(expos, axis=1)
        if after is not None:
            pn2[b] = jnp.concatenate(lates, axis=1)
        valid = b * fr + row < length
        r2[b] = jnp.where(valid, jnp.where(col // head == 0, inverse[0], inverse[1]), 0.0)

    def ahead_mix(b):
        here = pl.ds(b * fr, fr)
        mixed = dot(p2[b], jnp.concatenate([v2a[here, :], v2b[here, :]], axis=0))
        if b < n - 1:
            there = pl.ds((b + 1) * fr, tail)
            extra = dot(pn2[b], jnp.concatenate([v2a[there, :], v2b[there, :]], axis=0))
            mixed = jnp.concatenate([mixed[: fr - tail], mixed[fr - tail :] + extra], axis=0)
        ctx2s[b * fr : (b + 1) * fr, :] = (mixed * r2[b]).astype(jnp.bfloat16)

    with mark("y_out0"):
        out_block(0)
    with mark("y_out1"):
        out_block(1)
    with mark("ya_chain41"):
        chain(4, 1)
    with mark("y_out2"):
        out_block(2)
    with mark("y_out3"):
        out_block(3)
    with mark("yb_agf30"):
        ag_forward(3, 0)
    with mark("yc_chainend3"):
        chain_end(3)
    for g in range(groups):
        with mark(f"yd_proj{g}"):
            nx_copy(g, True).wait_recv()
            project(nbuf2, w2, g, (q2, k2a, k2b), None)
            if g:
                ahead(2 * g - 1)
            ahead(2 * g)
        if g == 1:
            with mark("ye_agf31"):
                ag_forward(3, 1)
        if g == 2:
            with mark("yf_chain42"):
                chain(4, 2)
    with mark("yg_last"):
        ahead(n - 1)
    with mark("yh_agf32"):
        ag_forward(3, 2)
    with mark("yi_chainend4"):
        chain_end(4)
    with mark("yj_mix2"):
        for g in range(groups):
            project(nbuf2, w2, g, None, (v2a, v2b))
        for b in range(n):
            ahead_mix(b)
    with mark("yk_agp3"):
        ag_partner(3)

    def back_copy(d):
        b = lax.rem(t + d, n)
        return pltpu.make_async_remote_copy(
            src_ref=ctx2s.at[at_rows(b, fr), :],
            dst_ref=ctx2.at[:, at_cols(t)],
            send_sem=a2_send.at[0, d], recv_sem=a2_recv.at[0, d],
            device_id=(b, z), device_id_type=MESH,
        )

    def back_wait(d):
        b = lax.rem(t + n - d, n)
        pltpu.make_async_remote_copy(
            src_ref=ctx2s.at[at_rows(b, fr), :],
            dst_ref=ctx2.at[:, at_cols(b)],
            send_sem=a2_send.at[0, d], recv_sem=a2_recv.at[0, d],
            device_id=(b, z), device_id_type=MESH,
        ).wait_recv()

    def term(zz):
        return dot(cott[at_rows(zz, rows), :], ctx2s[...])

    def z_copy(d):
        to = lax.rem(z + d, nz)
        return pltpu.make_async_remote_copy(
            src_ref=gsend.at[d], dst_ref=grecv.at[d],
            send_sem=z_send.at[d], recv_sem=z_recv.at[d],
            device_id=(t, to), device_id_type=MESH,
        )

    with mark("z_terms"):
        for d in range(1, nz):
            gsend[d] = term(lax.rem(z + d, nz)).astype(jnp.bfloat16)
            z_copy(d).start()
        for d in range(1, n):
            back_copy(d).start()
        ctx2[:, at_cols(t)] = ctx2s[at_rows(t, fr), :]
        total = term(z)
    with mark("za_zwait"):
        for d in range(1, nz):
            z_copy(d).wait_recv()
            total = total + grecv[d].astype(jnp.float32)
        gsum[...] = total

    def g_copy(d):
        b = lax.rem(t + d, n)
        return pltpu.make_async_remote_copy(
            src_ref=gsum.at[at_rows(b, part), :],
            dst_ref=wgr.at[:, pl.ds(mine, cols)],
            send_sem=a2_send.at[1, d], recv_sem=a2_recv.at[1, d],
            device_id=(b, z), device_id_type=MESH,
        )

    for d in range(1, n):
        g_copy(d).start()
    with mark("zb_back"):
        wgr[:, pl.ds(mine, cols)] = gsum[at_rows(t, part), :]
        for d in range(1, n):
            back_wait(d)
        context_ref[...] = ctx2[...]
    with mark("zc_gwait"):
        for d in range(1, n):
            b = lax.rem(t + n - d, n)
            pltpu.make_async_remote_copy(
                src_ref=gsum.at[at_rows(b, part), :],
                dst_ref=wgr.at[:, at_cols(b)],
                send_sem=a2_send.at[1, d], recv_sem=a2_recv.at[1, d],
                device_id=(b, z), device_id_type=MESH,
            ).wait_recv()
        grad_ref[...] = wgr[...]
    with mark("zd_sent"):
        for which in range(4):
            ag_sent(which)
        for which in range(5):
            chain_sent(which)
        for g in range(groups):
            nx_copy(g, False).wait_send()
            for m in range(1, 8):
                cx_copy(g, m).wait_send()
        for d in range(1, n):
            back_copy(d).wait_send()
            g_copy(d).wait_send()
        for d in range(1, nz):
            z_copy(d).wait_send()


def hand_out(context_ref, grad_ref, context_out, grad_out):
    context_out[...] = context_ref[...]
    grad_out[...] = grad_ref[...]


def by_heads(
    n, nz, frames, gain_one, qkv_one, out_one, gain_two, qkv_two, lengths, left_counts, cotangent
):
    _, fr, width = frames.shape
    cols = width // n
    rows = width // nz
    span = n * fr
    tail = -(-RIGHT // 16) * 16
    per = HEADS // n
    vmem = pl.BlockSpec(memory_space=pltpu.VMEM)
    smem = pl.BlockSpec(memory_space=pltpu.SMEM)
    hbm = pl.BlockSpec(memory_space=pltpu.HBM)
    bf16, f32 = jnp.bfloat16, jnp.float32
    dma = pltpu.SemaphoreType.DMA
    large = (
        frames[0], gain_one[None], qkv_one, out_one, gain_two[None], qkv_two, cotangent[0],
    )
    large = [pltpu.with_memory_space_constraint(value, pltpu.HBM) for value in large]
    context, grad = pl.pallas_call(
        functools.partial(heads_kernel, n, nz),
        out_shape=(
            jax.ShapeDtypeStruct((fr, width), bf16),
            jax.ShapeDtypeStruct((rows // n, width), f32),
        ),
        in_specs=[hbm] * 6 + [smem] * 2 + [hbm],
        out_specs=(vmem, vmem),
        scratch_shapes=[
            pltpu.VMEM((n, fr, width), bf16),
            pltpu.VMEM((n, fr, width), bf16),
            pltpu.VMEM((n, fr, width), bf16),
            pltpu.VMEM((width, 3 * cols), bf16),
            pltpu.VMEM((width, 3 * cols), bf16),
            pltpu.VMEM((width, width), bf16),
            pltpu.VMEM((fr, width), bf16),
            pltpu.VMEM((width, span), bf16),
            pltpu.VMEM((2, width), f32),
            *[pltpu.VMEM((span, cols), bf16)] * 5,
            pltpu.VMEM((n, fr, per * (LEFT_MAX + 1) * fr), bf16),
            pltpu.VMEM((n, fr, cols), f32),
            pltpu.VMEM((span, cols), bf16),
            pltpu.VMEM((n // 2, fr, width), bf16),
            *[pltpu.VMEM((span, cols), bf16)] * 5,
            pltpu.VMEM((n, fr, per * fr), bf16),
            pltpu.VMEM((n, tail, per * tail), bf16),
            pltpu.VMEM((n, fr, cols), f32),
            pltpu.VMEM((span, cols), bf16),
            pltpu.VMEM((fr, width), bf16),
            pltpu.VMEM((nz, rows, cols), bf16),
            pltpu.VMEM((nz, rows, cols), bf16),
            pltpu.VMEM((rows, cols), f32),
            pltpu.VMEM((rows // n, width), f32),
            dma((11,)),
            dma((4, 11)),
            dma((4, 11)),
            dma((5, 2, nz, 2)),
            dma((5, nz, 2)),
            dma((n // 2, 8)),
            dma((n // 2, 8)),
            dma((n // 2,)),
            dma((n // 2,)),
            dma((2, n)),
            dma((2, n)),
            dma((nz,)),
            dma((nz,)),
        ],
        compiler_params=pltpu.CompilerParams(
            collective_id=0, has_side_effects=True, vmem_limit_bytes=44 * 1024 * 1024
        ),
    )(*large[:6], lengths, left_counts, large[6])
    context, grad = pl.pallas_call(
        hand_out,
        out_shape=(
            jax.ShapeDtypeStruct((fr, width), bf16),
            jax.ShapeDtypeStruct((rows // n, width), f32),
        ),
        in_specs=[vmem, vmem],
        out_specs=(vmem, vmem),
        compiler_params=pltpu.CompilerParams(vmem_limit_bytes=4 * 1024 * 1024),
    )(context, grad)
    return (context[None], grad)


def solution(mesh):
    n_tm = mesh.shape["tm"]
    even = n_tm == 2 * CHIPS and mesh.shape["fsdp"] == CHIPS and HEADS == 2 * n_tm
    chosen = functools.partial(by_heads, n_tm, mesh.shape["fsdp"]) if even else on_device
    in_specs = (
        P("fsdp", "tm", None),
        P(),
        P("fsdp", None),
        P("fsdp", None),
        P(),
        P("fsdp", None),
        P("fsdp"),
        P("fsdp"),
        P("fsdp", "tm", None),
    )
    out_specs = (P("fsdp", "tm", None), P(("tm", "fsdp"), None))
    return jax.shard_map(
        chosen, mesh=mesh, in_specs=in_specs, out_specs=out_specs, check_vma=False
    )
```

time: 70.6 us -> 62.5 us (0.89)
  Pallas kernels: 68.5 us -> 60.4 us
    pallas_call x1, Pallas kernels: 66.8 us -> 59.7 us  [by_heads(): pl.pallas_call(functools.partial(heads_kernel, n, nz), out_shape=(jax.Sha...]
    pallas_call x1, Pallas kernels: 1.74 us -> 0.77 us  [by_heads(): pl.pallas_call(hand_out, out_shape=(jax.ShapeDtypeStruct((fr, width), bf1...]
where the time goes in v1:
time: 62.5 us; the launch traced here: 62.4 us
  Pallas kernels  60.4 us (97%)
  between operations  1.93 us (3%)
    pallas_call x1, Pallas kernels, by_heads(): pl.pallas_call(functools.partial(heads_kernel, n, nz), out_shape=(jax.Sha...  59.7 us

profile of v1, /device:TPU:0, one launch (start us, length us, event | category | flops | bytes accessed | tf_op | source)
XLA Modules:
  0.0 62.4 jit_solution(6405183080584243246)
XLA Ops:
  1.9 59.7 %shard_map.104 = (bf16[128,1024]{1,0:T(8,128)(2,1)S(1)}, f32[32,1024]{1,0:T(8,128)S(1)}) custom-call(bf16[128,1024]{1,0:T(8,128)(2,1)} %bitcast.5, f32[1,1024]{1,0:T(1,128)} %bitcast.7, bf16[256,3072]{1,0:T(8,128)(2,1)} %qkv_one_ref.1, bf16[256,1024]{1,0:T(8,128)(2,1)} %out_one_ref.1, f32[1,1024]{1,0:T(1,128)} %bitcast.8, bf16[256,3072]{1,0:T(8,128)(2,1)} %qkv_two_ref.1, ...), custom_call_target="tpu_custom_call" | custom-call | tf_op jit(solution)/shard_map/pallas_call | solution.py:787
  61.6 0.8 %shard_map.105 = (bf16[128,1024]{1,0:T(8,128)(2,1)}, f32[32,1024]{1,0:T(8,128)}) custom-call(bf16[128,1024]{1,0:T(8,128)(2,1)S(1)} %get-tuple-element.6.context_ref, f32[32,1024]{1,0:T(8,128)S(1)} %get-tuple-element.7.grad_ref), custom_call_target="tpu_custom_call" | custom-call | tf_op jit(solution)/shard_map/pallas_call | solution.py:838

commit v2 on v1

--- a/solution.py
+++ b/solution.py
@@ -125,9 +125,8 @@
     fbuf, nbuf, nbuf2, w1, w2, wo, cotv, cott, gains,
     q1, k1a, k1b, v1a, v1b, p1, r1, ctx1s, ctxall,
     q2, k2a, k2b, v2a, v2b, p2, pn2, r2, ctx2s, ctx2,
-    gsend, grecv, gsum, wgr,
-    local_sem, ag_send, ag_recv, ch_send, ch_recv, cx_send, cx_recv, nx_send, nx_recv,
-    a2_send, a2_recv, z_send, z_recv,
+    gsend, grecv,
+    local_sem, ag_send, ag_recv, ch_recv, cx_recv, nx_recv, one_sem, far_sem,
 ):
     t = lax.axis_index("tm")
     z = lax.axis_index("fsdp")
@@ -174,78 +173,94 @@
 
     get_frames = load(frames_ref, fbuf.at[t], 0)
     get_wo = load(out_one_ref, wo.at[pl.ds(0, rows), :], 1)
-    get_w1 = [load_cols(qkv_one_ref, w1, j, 2 + j) for j in range(3)]
-    get_w2 = [load_cols(qkv_two_ref, w2, j, 5 + j) for j in range(3)]
-    get_cot = load(cot_ref, cotv, 8)
-    get_gains = [load(gain_one_ref, gains.at[0:1], 9), load(gain_two_ref, gains.at[1:2], 10)]
+    get_w1 = [load_cols(qkv_one_ref, w1, j, 2 + j // 2) for j in range(3)]
+    get_w2 = [load_cols(qkv_two_ref, w2, j, 4) for j in range(3)]
+    get_cot = load(cot_ref, cotv, 5)
+    get_gains = [load(gain_one_ref, gains.at[0:1], 6), load(gain_two_ref, gains.at[1:2], 6)]
     for copy in [get_frames, get_wo, *get_w1, *get_gains, get_cot, *get_w2]:
         copy.start()
 
+    def loaded(view, index):
+        load(view, view, index).wait()
+
+    CHAIN, CROSS, PAIR, BACK, GRAD, BACK_IN, GRAD_IN = (one_sem.at[i] for i in range(7))
+
+    def sent(sem, view):
+        pltpu.make_async_remote_copy(
+            src_ref=view, dst_ref=view, send_sem=sem, recv_sem=sem,
+            device_id=(flip(t, 1), z), device_id_type=MESH,
+        ).wait_send()
+
+    def received(sem, view):
+        pltpu.make_async_remote_copy(
+            src_ref=view, dst_ref=view, send_sem=sem, recv_sem=sem,
+            device_id=(flip(t, 1), z), device_id_type=MESH,
+        ).wait_recv()
+
     half = rows // 2
+
+    NEAR, NEXT, FAR = 0, 1, 2
 
     def chain_view(which, shard, h, at):
         place = lax.rem(shard - at + nz, nz) if which == 0 else shard
-        span = pl.ds(pl.multiple_of(place * rows + h * half, half), half)
+        if h is None:
+            span = at_rows(place, rows)
+        else:
+            span = pl.ds(pl.multiple_of(place * rows + h * half, half), half)
         if which == 0:
             return wo.at[span, pl.ds(mine, cols)]
         wide = pl.ds(0, 2 * cols) if which in (1, 3) else pl.ds(2 * cols, cols)
         return (w1 if which < 3 else w2).at[span, wide]
 
-    def chain_copy(which, step, up, h):
-        shard = z - step if up else z + step
-        shard = jnp.clip(shard, 0, nz - 1)
-        to = jnp.clip(z + 1 if up else z - 1, 0, nz - 1)
-        return pltpu.make_async_remote_copy(
-            src_ref=chain_view(which, shard, h, z),
-            dst_ref=chain_view(which, shard, h, to),
-            send_sem=ch_send.at[which, 0 if up else 1, step, h],
-            recv_sem=ch_recv.at[which, shard, h],
-            device_id=(t, to),
-            device_id_type=MESH,
-        )
-
-    def chain_wait(which, shard, h, other):
-        view = chain_view(which, shard, h, z)
-        pltpu.make_async_remote_copy(
-            src_ref=view,
-            dst_ref=view,
-            send_sem=ch_send.at[which, 0, 0, h],
-            recv_sem=ch_recv.at[which, shard, h],
-            device_id=(t, other),
-            device_id_type=MESH,
-        ).wait_recv()
-
-    def chain_cond(step, up):
-        if up:
-            return (z >= step) & (z < nz - 1)
-        return (z + step < nz) & (z > 0)
-
-    def chain(which, step, halves=(0, 1)):
-        for h in halves:
+    def chain_sem(which, shard, h, at):
+        apart = lax.rem(shard - at + nz, nz) - 1
+        if h is None:
+            return ch_recv.at[6 * (nz - 1) + (which - 3) * (nz - 1) + apart]
+        return ch_recv.at[(2 * which + h) * (nz - 1) + apart]
+
+    def pieces(which):
+        return (0, 1) if which < 3 else (None,)
+
+    def chain_cond(kind, up):
+        if kind == NEAR:
+            return z < nz - 1 if up else z > 0
+        if kind == NEXT:
+            return (z > 0) & (z < nz - 1)
+        return z == 0 if up else z == nz - 1
+
+    def chain_wait(which, shard, h):
+        received(chain_sem(which, shard, h, z), chain_view(which, shard, h, z))
+
+    def chain(which, kind, halves=None):
+        for h in halves or pieces(which):
             for up in (True, False):
-                @pl.when(chain_cond(step, up))
+                @pl.when(chain_cond(kind, up))
                 def _():
-                    copy = chain_copy(which, step, up, h)
-                    if step:
-                        chain_wait(which, z - step if up else z + step, h, z + 1 if up else z - 1)
-                    copy.start()
+                    way = 1 if up else -1
+                    shard = z - way if kind == NEXT else z
+                    to = (nz - 1 if up else 0) if kind == FAR else z + way
+                    shard, to = jnp.clip(shard, 0, nz - 1), jnp.clip(to, 0, nz - 1)
+                    if kind == NEXT:
+                        chain_wait(which, shard, h)
+                    pltpu.make_async_remote_copy(
+                        src_ref=chain_view(which, shard, h, z),
+                        dst_ref=chain_view(which, shard, h, to),
+                        send_sem=CHAIN,
+                        recv_sem=chain_sem(which, shard, h, to),
+                        device_id=(t, to),
+                        device_id_type=MESH,
+                    ).start()
 
     def chain_end(which):
-        for edge, up in ((nz - 1, True), (0, False)):
-            @pl.when(z == edge)
-            def _():
-                for step in range(1, nz):
-                    for h in range(2):
-                        shard = edge - step if up else edge + step
-                        chain_wait(which, shard, h, edge - 1 if up else edge + 1)
-
-    def chain_sent(which):
-        for step in range(nz - 1):
-            for up in (True, False):
-                for h in range(2):
-                    @pl.when(chain_cond(step, up))
-                    def _():
-                        chain_copy(which, step, up, h).wait_send()
+        for apart in range(1, nz):
+            for way in (1, -1):
+                ends = (z == nz - 1) if way == 1 else (z == 0)
+                there = z - way * apart
+                inside = (there >= 0) & (there < nz)
+                @pl.when(inside & ends if apart == 1 else inside)
+                def _():
+                    for h in pieces(which):
+                        chain_wait(which, jnp.clip(there, 0, nz - 1), h)
 
     def ag_view(which, index, piece):
         if which == 0:
@@ -265,23 +280,25 @@
         (2, None, 1), (4, None, 1), (6, 0, 1), (6, 1, 1),
     )
 
+    shared = {1: 0, 3: 1, 2: 2, 4: 3, 5: 4, 6: 5, 0: 6}
+
+    def ag_sem(which, slot):
+        if which == 0:
+            return ag_recv.at[shared.get(slot, 7 if slot < 9 else 8)]
+        return ag_recv.at[9 + 7 * (which - 1) + shared.get(slot, 6)]
+
     def ag_copy(which, slot):
         block, piece, to = slots[slot]
         view = ag_view(which, flip(t, block), piece)
         return pltpu.make_async_remote_copy(
             src_ref=view, dst_ref=view,
-            send_sem=ag_send.at[which, slot], recv_sem=ag_recv.at[which, slot],
+            send_sem=ag_send.at[which], recv_sem=ag_sem(which, slot),
             device_id=(flip(t, to), z), device_id_type=MESH,
         )
 
     def ag_wait(which, slot):
         block, piece, to = slots[slot]
-        view = ag_view(which, flip(t, block ^ to), piece)
-        pltpu.make_async_remote_copy(
-            src_ref=view, dst_ref=view,
-            send_sem=ag_send.at[which, slot], recv_sem=ag_recv.at[which, slot],
-            device_id=(flip(t, to), z), device_id_type=MESH,
-        ).wait_recv()
+        received(ag_sem(which, slot), ag_view(which, flip(t, block ^ to), piece))
 
     def ag_start(which):
         for slot in (1, 3, 2, 4, 0):
@@ -294,13 +311,18 @@
             ag_wait(which, waits)
             ag_copy(which, slot).start()
 
+    def ag_many(which, blocks):
+        if which == 0:
+            return fbuf.at[0:blocks]
+        first = (0, 0, rows, 0)[which]
+        size = width - rows if which == 2 else width // 2
+        return (wo if which == 2 else cott).at[first : first + size, 0 : blocks * cols]
+
     def ag_partner(which):
-        for slot in (0, 7, 8, 9, 10):
-            ag_wait(which, slot)
+        received(ag_sem(which, 0), ag_many(which, 4))
 
     def ag_sent(which):
-        for slot in range(len(slots)):
-            ag_copy(which, slot).wait_send()
+        sent(ag_send.at[which], ag_many(which, n - 1))
 
     def normed(index):
         nbuf[index] = norm_rows(fbuf[index], gains[0:1, :])
@@ -342,18 +364,37 @@
         get_frames.wait()
     ag_start(0)
     get_wo.wait()
-    chain(0, 0)
-    with mark("c_w1local"):
-        get_w1[0].wait()
-        get_w1[1].wait()
-    chain(1, 0, (0,))
+    chain(0, NEAR)
+    inner = (z > 0) & (z < nz - 1)
+    lower = z < nz // 2
+
+    @pl.when(inner)
+    def _():
+        other = jnp.clip(jnp.where(lower, z + 1, z - 1), 0, nz - 1)
+        pl.semaphore_signal(far_sem, inc=1, device_id=(t, other), device_id_type=MESH)
+
+    loaded(w1.at[own_rows, 0 : 2 * cols], 2)
+    chain(1, NEAR, (0,))
     with mark("d_norm"):
-        for copy in get_gains:
-            copy.wait()
+        loaded(gains, 6)
         normed(t)
-    with mark("e_chain01"):
-        chain(0, 1)
-    chain(1, 0, (1,))
+    with mark("e_far"):
+        @pl.when(inner)
+        def _():
+            edge = jnp.clip(jnp.where(lower, z - 1, z + 1), 0, nz - 1)
+            pl.semaphore_wait(far_sem, 1)
+            pl.semaphore_signal(far_sem, inc=1, device_id=(t, edge), device_id_type=MESH)
+
+    with mark("e_next0"):
+        chain(0, NEXT)
+    chain(1, NEAR, (1,))
+    with mark("e_edge"):
+        @pl.when((z == 0) | (z == nz - 1))
+        def _():
+            pl.semaphore_wait(far_sem, 1)
+
+    chain(0, FAR)
+    chain(1, FAR)
     with mark("f_agf00"):
         ag_forward(0, 0)
     with mark("g_turn"):
@@ -366,38 +407,38 @@
                 )
         ag_wait(0, 0)
         normed(flip(t, 1))
-    with mark("h_chain02"):
-        chain(0, 2)
     with mark("i_agf01"):
         ag_forward(0, 1)
-    with mark("j_chain11"):
-        chain(1, 1)
+    with mark("j_next1a"):
+        chain(1, NEXT, (0,))
     with mark("k_chainend0"):
         chain_end(0)
     ag_start(2)
     with mark("l_norms"):
         normed(flip(t, 2))
         normed(flip(t, 4))
-    with mark("m_chain12"):
-        chain(1, 2)
-    get_w1[2].wait()
-    chain(2, 0)
+    with mark("m_next1b"):
+        chain(1, NEXT, (1,))
+    loaded(w1.at[own_rows, 2 * cols : 3 * cols], 3)
+    chain(2, NEAR)
+    chain(2, FAR)
     with mark("n_agf02"):
         ag_forward(0, 2)
     with mark("o_norms"):
-        ag_wait(0, 7)
+        received(ag_sem(0, 7), ag_many(0, 2))
         normed(flip(t, 3))
-        ag_wait(0, 8)
         normed(flip(t, 5))
         normed(flip(t, 6))
-    with mark("p_agf20"):
+    with mark("q_agf20"):
         ag_forward(2, 0)
-    with mark("q_norm"):
-        ag_wait(0, 9)
-        ag_wait(0, 10)
+    ag_start(1)
+    with mark("p_norm"):
+        received(ag_sem(0, 9), ag_many(0, 1))
         normed(flip(t, 7))
     with mark("r_chainend1"):
         chain_end(1)
+    with mark("ra_next2"):
+        chain(2, NEXT)
     with mark("s_projqk"):
         for pair in range(groups):
             project(nbuf, w1, pair, (q1, k1a, k1b), None)
@@ -451,33 +492,25 @@
     with mark("t_soft0"):
         causal(0)
         causal(1)
-    with mark("ta_chain21"):
-        chain(2, 1)
-    with mark("tb_agf21"):
+    with mark("ta_agf21"):
         ag_forward(2, 1)
     with mark("t_soft1"):
         causal(2)
         causal(3)
-    with mark("tc_chain22"):
-        chain(2, 2, (0,))
     with mark("td_agf22"):
         ag_forward(2, 2)
-    ag_start(1)
     with mark("t_soft2"):
         causal(4)
         causal(5)
-    with mark("te_chain22"):
-        chain(2, 2, (1,))
-    for copy in get_w2:
-        copy.wait()
-    chain(3, 0)
-    with mark("t_soft3"):
         causal(6)
         causal(7)
     with mark("u_agf10"):
         ag_forward(1, 0)
+    loaded(w2.at[own_rows, :], 4)
+    chain(3, NEAR)
     with mark("v_chainend2"):
         chain_end(2)
+    chain(3, FAR)
     with mark("w_projv"):
         for pair in range(groups):
             project(nbuf, w1, pair, None, (v1a, v1b))
@@ -497,75 +530,56 @@
             dst = src
         return pltpu.make_async_remote_copy(
             src_ref=src, dst_ref=dst,
-            send_sem=cx_send.at[g, m], recv_sem=cx_recv.at[g, m],
+            send_sem=CROSS, recv_sem=cx_recv.at[3 * g + (0, 2, 0, 0, 1, 1, 2, 2)[m]],
             device_id=(to, z), device_id_type=MESH,
         )
 
-    def cx_wait(g, m):
-        to = flip(t, (m, 4, 2)[max(m - 5, 0)])
-        if m < 6:
-            view = ctxall.at[g, :, at_cols(turned(to))]
-        else:
-            view = ctxall.at[
-                g,
-                pl.ds((m - 6) * (fr // 2), fr // 2),
-                pl.ds(pl.multiple_of(turned(flip(t, 6) // 2 * 2) * cols, 2 * cols), 2 * cols),
-            ]
-        pltpu.make_async_remote_copy(
-            src_ref=view, dst_ref=view,
-            send_sem=cx_send.at[g, m], recv_sem=cx_recv.at[g, m],
-            device_id=(to, z), device_id_type=MESH,
-        ).wait_recv()
+    def cx_wait(g, kind):
+        received(cx_recv.at[3 * g + kind], ctxall.at[g, :, 0 : (2, 2, 3)[kind] * cols])
 
     def cx_forward(g):
-        cx_wait(g, 2)
-        cx_wait(g, 3)
+        cx_wait(g, 0)
         cx_copy(g, 6).start()
-        cx_wait(g, 4)
-        cx_wait(g, 5)
+        cx_wait(g, 1)
         cx_copy(g, 7).start()
+
+    def cx_send(g):
+        for m in (2, 4, 3, 5, 1):
+            cx_copy(g, m).start()
 
     with mark("x_mix"):
         for g in range(groups):
             causal_mix(2 * g)
             causal_mix(2 * g + 1)
-            for m in (2, 4, 3, 5, 1):
-                cx_copy(g, m).start()
+            if g < 3:
+                cx_send(g)
             ctxall[g, :, at_cols(turned(t))] = ctx1s[at_rows(2 * g + core, fr), :]
+    chain(4, NEAR)
     with mark("xa_agf11"):
         ag_forward(1, 1)
-    with mark("xb_chain31"):
-        chain(3, 1)
+    with mark("xb_next3"):
+        chain(3, NEXT)
+    chain(4, FAR)
+    with mark("xd_fwd0"):
+        cx_forward(0)
+    cx_send(3)
     with mark("xc_agf12"):
         ag_forward(1, 2)
-    with mark("xd_fwd0"):
-        cx_forward(0)
-    with mark("xe_agp2"):
+    with mark("xe_fwd1"):
+        cx_forward(1)
+    with mark("xf_agp2"):
         ag_partner(2)
-    with mark("xf_fwd1"):
-        cx_forward(1)
-    with mark("xg_chain32"):
-        chain(3, 2)
-    chain(4, 0)
-    with mark("xh_fwd2"):
-        cx_forward(2)
-    with mark("xi_fwd3"):
-        cx_forward(3)
-    ag_start(3)
-    with mark("xj_agp1"):
-        ag_partner(1)
 
     def nx_copy(g, other):
         view = nbuf2.at[2 * g + (1 - core if other else core)]
         return pltpu.make_async_remote_copy(
             src_ref=view, dst_ref=view,
-            send_sem=nx_send.at[g], recv_sem=nx_recv.at[g],
+            send_sem=PAIR, recv_sem=nx_recv.at[g],
             device_id=(flip(t, 1), z), device_id_type=MESH,
         )
 
     def out_block(g):
-        for m in (1, 6, 7):
-            cx_wait(g, m)
+        cx_wait(g, 2)
         b = 2 * g + core
         mixed = dot(ctxall[g], wo[...])
         hidden = (fbuf[b].astype(jnp.float32) + mixed).astype(jnp.bfloat16)
@@ -635,37 +649,47 @@
             mixed = jnp.concatenate([mixed[: fr - tail], mixed[fr - tail :] + extra], axis=0)
         ctx2s[b * fr : (b + 1) * fr, :] = (mixed * r2[b]).astype(jnp.bfloat16)
 
+    def second(g):
+        nx_copy(g, True).wait_recv()
+        project(nbuf2, w2, g, (q2, k2a, k2b), None)
+        if g:
+            ahead(2 * g - 1)
+        ahead(2 * g)
+
     with mark("y_out0"):
         out_block(0)
+    with mark("ya_fwd2"):
+        cx_forward(2)
+    with mark("yb_next4"):
+        chain(4, NEXT)
     with mark("y_out1"):
         out_block(1)
-    with mark("ya_chain41"):
-        chain(4, 1)
+    with mark("yc_fwd3"):
+        cx_forward(3)
+    ag_start(3)
+    with mark("yd_chainend3"):
+        chain_end(3)
+    with mark("ye_second0"):
+        second(0)
     with mark("y_out2"):
         out_block(2)
+    with mark("ye_second1"):
+        second(1)
+    with mark("yg_agf30"):
+        ag_forward(3, 0)
     with mark("y_out3"):
         out_block(3)
-    with mark("yb_agf30"):
-        ag_forward(3, 0)
-    with mark("yc_chainend3"):
-        chain_end(3)
-    for g in range(groups):
-        with mark(f"yd_proj{g}"):
-            nx_copy(g, True).wait_recv()
-            project(nbuf2, w2, g, (q2, k2a, k2b), None)
-            if g:
-                ahead(2 * g - 1)
-            ahead(2 * g)
-        if g == 1:
-            with mark("ye_agf31"):
-                ag_forward(3, 1)
-        if g == 2:
-            with mark("yf_chain42"):
-                chain(4, 2)
-    with mark("yg_last"):
+    with mark("yh_agf31"):
+        ag_forward(3, 1)
+    with mark("ye_second2"):
+        second(2)
+    with mark("yk_agf32"):
+        ag_forward(3, 2)
+    with mark("yf_agp1"):
+        ag_partner(1)
+    with mark("ye_second3"):
+        second(3)
         ahead(n - 1)
-    with mark("yh_agf32"):
-        ag_forward(3, 2)
     with mark("yi_chainend4"):
         chain_end(4)
     with mark("yj_mix2"):
@@ -673,92 +697,62 @@
             project(nbuf2, w2, g, None, (v2a, v2b))
         for b in range(n):
             ahead_mix(b)
-    with mark("yk_agp3"):
+    with mark("yl_agp3"):
         ag_partner(3)
 
     def back_copy(d):
-        b = lax.rem(t + d, n)
         return pltpu.make_async_remote_copy(
-            src_ref=ctx2s.at[at_rows(b, fr), :],
+            src_ref=ctx2s.at[at_rows(lax.rem(t + d, n), fr), :],
             dst_ref=ctx2.at[:, at_cols(t)],
-            send_sem=a2_send.at[0, d], recv_sem=a2_recv.at[0, d],
-            device_id=(b, z), device_id_type=MESH,
+            send_sem=BACK, recv_sem=BACK_IN,
+            device_id=(lax.rem(t + d, n), z), device_id_type=MESH,
         )
 
-    def back_wait(d):
-        b = lax.rem(t + n - d, n)
-        pltpu.make_async_remote_copy(
-            src_ref=ctx2s.at[at_rows(b, fr), :],
-            dst_ref=ctx2.at[:, at_cols(b)],
-            send_sem=a2_send.at[0, d], recv_sem=a2_recv.at[0, d],
-            device_id=(b, z), device_id_type=MESH,
-        ).wait_recv()
-
-    def term(zz):
-        return dot(cott[at_rows(zz, rows), :], ctx2s[...])
-
-    def z_copy(d):
-        to = lax.rem(z + d, nz)
+    def grad_copy(m, d):
+        to = lax.rem(t + d, n)
         return pltpu.make_async_remote_copy(
-            src_ref=gsend.at[d], dst_ref=grecv.at[d],
-            send_sem=z_send.at[d], recv_sem=z_recv.at[d],
-            device_id=(t, to), device_id_type=MESH,
+            src_ref=gsend.at[m, at_rows(to, part), :],
+            dst_ref=grecv.at[m, :, at_cols(t)],
+            send_sem=GRAD, recv_sem=GRAD_IN,
+            device_id=(to, flip(z, m) if m else z), device_id_type=MESH,
         )
 
     with mark("z_terms"):
-        for d in range(1, nz):
-            gsend[d] = term(lax.rem(z + d, nz)).astype(jnp.bfloat16)
-            z_copy(d).start()
+        for m in (3, 2, 1, 0):
+            zz = flip(z, m) if m else z
+            gsend[m] = dot(cott[at_rows(zz, rows), :], ctx2s[...]).astype(jnp.bfloat16)
+            for d in range(1 if m == 0 else 0, n):
+                grad_copy(m, d).start()
+        grecv[0, :, at_cols(t)] = gsend[0, at_rows(t, part), :]
         for d in range(1, n):
             back_copy(d).start()
         ctx2[:, at_cols(t)] = ctx2s[at_rows(t, fr), :]
-        total = term(z)
-    with mark("za_zwait"):
-        for d in range(1, nz):
-            z_copy(d).wait_recv()
-            total = total + grecv[d].astype(jnp.float32)
-        gsum[...] = total
-
-    def g_copy(d):
-        b = lax.rem(t + d, n)
-        return pltpu.make_async_remote_copy(
-            src_ref=gsum.at[at_rows(b, part), :],
-            dst_ref=wgr.at[:, pl.ds(mine, cols)],
-            send_sem=a2_send.at[1, d], recv_sem=a2_recv.at[1, d],
-            device_id=(b, z), device_id_type=MESH,
-        )
-
-    for d in range(1, n):
-        g_copy(d).start()
+    with mark("za_grads"):
+        received(GRAD_IN, ctx2s.at[0 : (n * nz - 1) * part, :])
+        total = grecv[0].astype(jnp.float32)
+        for m in range(1, nz):
+            total = total + grecv[m].astype(jnp.float32)
+        grad_ref[...] = total
     with mark("zb_back"):
-        wgr[:, pl.ds(mine, cols)] = gsum[at_rows(t, part), :]
-        for d in range(1, n):
-            back_wait(d)
+        received(BACK_IN, ctx2.at[:, 0 : (n - 1) * cols])
         context_ref[...] = ctx2[...]
-    with mark("zc_gwait"):
-        for d in range(1, n):
-            b = lax.rem(t + n - d, n)
-            pltpu.make_async_remote_copy(
-                src_ref=gsum.at[at_rows(b, part), :],
-                dst_ref=wgr.at[:, at_cols(b)],
-                send_sem=a2_send.at[1, d], recv_sem=a2_recv.at[1, d],
-                device_id=(b, z), device_id_type=MESH,
-            ).wait_recv()
-        grad_ref[...] = wgr[...]
     with mark("zd_sent"):
         for which in range(4):
             ag_sent(which)
-        for which in range(5):
-            chain_sent(which)
-        for g in range(groups):
-            nx_copy(g, False).wait_send()
-            for m in range(1, 8):
-                cx_copy(g, m).wait_send()
-        for d in range(1, n):
-            back_copy(d).wait_send()
-            g_copy(d).wait_send()
-        for d in range(1, nz):
-            z_copy(d).wait_send()
+        whole = 7 * rows * cols // width
+
+        @pl.when((z == 0) | (z == nz - 1))
+        def _():
+            sent(CHAIN, cott.at[0 : 2 * whole, :])
+
+        @pl.when((z > 0) & (z < nz - 1))
+        def _():
+            sent(CHAIN, cott.at[0 : 4 * whole, :])
+
+        sent(CROSS, cott.at[0 : 7 * groups * fr * cols // width, :])
+        sent(PAIR, nbuf2.at[0:groups])
+        sent(BACK, ctx2.at[:, 0 : (n - 1) * cols])
+        sent(GRAD, ctx2s.at[0 : (n * nz - 1) * part, :])
 
 
 def hand_out(context_ref, grad_ref, context_out, grad_out):
@@ -814,22 +808,15 @@
             pltpu.VMEM((span, cols), bf16),
             pltpu.VMEM((fr, width), bf16),
             pltpu.VMEM((nz, rows, cols), bf16),
-            pltpu.VMEM((nz, rows, cols), bf16),
-            pltpu.VMEM((rows, cols), f32),
-            pltpu.VMEM((rows // n, width), f32),
-            dma((11,)),
-            dma((4, 11)),
-            dma((4, 11)),
-            dma((5, 2, nz, 2)),
-            dma((5, nz, 2)),
-            dma((n // 2, 8)),
-            dma((n // 2, 8)),
+            pltpu.VMEM((nz, rows // n, width), bf16),
+            dma((7,)),
+            dma((4,)),
+            dma((30,)),
+            dma((8 * (nz - 1),)),
+            dma((3 * n // 2,)),
             dma((n // 2,)),
-            dma((n // 2,)),
-            dma((2, n)),
-            dma((2, n)),
-            dma((nz,)),
-            dma((nz,)),
+            dma((7,)),
+            pltpu.SemaphoreType.REGULAR,
         ],
         compiler_params=pltpu.CompilerParams(
             collective_id=0, has_side_effects=True, vmem_limit_bytes=44 * 1024 * 1024

time: 62.5 us -> 57.2 us (0.915)
  Pallas kernels: 60.4 us -> 55.1 us
    pallas_call x1, Pallas kernels: 59.7 us -> 54.4 us  [by_heads(): pl.pallas_call(functools.partial(heads_kernel, n, nz), out_shape=(jax.Sha...]
where the time goes in v2:
time: 57.2 us; the launch traced here: 57.1 us
  Pallas kernels  55.1 us (96%)
  between operations  1.93 us (3%)
    pallas_call x1, Pallas kernels, by_heads(): pl.pallas_call(functools.partial(heads_kernel, n, nz), out_shape=(jax.Sha...  54.4 us

profile of v2, /device:TPU:0, one launch (start us, length us, event | category | flops | bytes accessed | tf_op | source)
XLA Modules:
  0.0 57.1 jit_solution(2237779692820034007)
XLA Ops:
  1.9 54.4 %shard_map.104 = (bf16[128,1024]{1,0:T(8,128)(2,1)S(1)}, f32[32,1024]{1,0:T(8,128)S(1)}) custom-call(bf16[128,1024]{1,0:T(8,128)(2,1)} %bitcast.5, f32[1,1024]{1,0:T(1,128)} %bitcast.7, bf16[256,3072]{1,0:T(8,128)(2,1)} %qkv_one_ref.1, bf16[256,1024]{1,0:T(8,128)(2,1)} %out_one_ref.1, f32[1,1024]{1,0:T(1,128)} %bitcast.8, bf16[256,3072]{1,0:T(8,128)(2,1)} %qkv_two_ref.1, ...), custom_call_target="tpu_custom_call" | custom-call | tf_op jit(solution)/shard_map/pallas_call | solution.py:781
  56.3 0.8 %shard_map.105 = (bf16[128,1024]{1,0:T(8,128)(2,1)}, f32[32,1024]{1,0:T(8,128)}) custom-call(bf16[128,1024]{1,0:T(8,128)(2,1)S(1)} %get-tuple-element.6.context_ref, f32[32,1024]{1,0:T(8,128)S(1)} %get-tuple-element.7.grad_ref), custom_call_target="tpu_custom_call" | custom-call | tf_op jit(solution)/shard_map/pallas_call | solution.py:825

commit v3 on v2

--- a/solution.py
+++ b/solution.py
@@ -125,8 +125,8 @@
     fbuf, nbuf, nbuf2, w1, w2, wo, cotv, cott, gains,
     q1, k1a, k1b, v1a, v1b, p1, r1, ctx1s, ctxall,
     q2, k2a, k2b, v2a, v2b, p2, pn2, r2, ctx2s, ctx2,
-    gsend, grecv,
-    local_sem, ag_send, ag_recv, ch_recv, cx_recv, nx_recv, one_sem, far_sem,
+    gsend, grecv, fsum, pbuf,
+    local_sem, ag_send, ag_recv, ch_recv, cx_recv, nx_recv, one_sem, far_sem, pre_sem,
 ):
     t = lax.axis_index("tm")
     z = lax.axis_index("fsdp")
@@ -262,13 +262,15 @@
                     for h in pieces(which):
                         chain_wait(which, jnp.clip(there, 0, nz - 1), h)
 
+    early = width * 5 // 8
+
     def ag_view(which, index, piece):
         if which == 0:
             if piece is None:
                 return fbuf.at[index]
             return fbuf.at[index, pl.ds(piece * (fr // 2), fr // 2), :]
         buf, first, size = (
-            None, (cott, 0, width // 2), (wo, rows, width - rows), (cott, width // 2, width // 2),
+            None, (cott, 0, early), (wo, rows, width - rows), (cott, early, width - early),
         )[which]
         if piece is None:
             return buf.at[pl.ds(first, size), at_cols(index)]
@@ -314,8 +316,8 @@
     def ag_many(which, blocks):
         if which == 0:
             return fbuf.at[0:blocks]
-        first = (0, 0, rows, 0)[which]
-        size = width - rows if which == 2 else width // 2
+        first = (0, 0, rows, early)[which]
+        size = (0, early, width - rows, width - early)[which]
         return (wo if which == 2 else cott).at[first : first + size, 0 : blocks * cols]
 
     def ag_partner(which):
@@ -439,6 +441,8 @@
         chain_end(1)
     with mark("ra_next2"):
         chain(2, NEXT)
+    loaded(w2.at[own_rows, :], 4)
+    chain(3, NEAR)
     with mark("s_projqk"):
         for pair in range(groups):
             project(nbuf, w1, pair, (q1, k1a, k1b), None)
@@ -506,8 +510,6 @@
         causal(7)
     with mark("u_agf10"):
         ag_forward(1, 0)
-    loaded(w2.at[own_rows, :], 4)
-    chain(3, NEAR)
     with mark("v_chainend2"):
         chain_end(2)
     chain(3, FAR)
@@ -554,12 +556,11 @@
             if g < 3:
                 cx_send(g)
             ctxall[g, :, at_cols(turned(t))] = ctx1s[at_rows(2 * g + core, fr), :]
-    chain(4, NEAR)
     with mark("xa_agf11"):
         ag_forward(1, 1)
     with mark("xb_next3"):
         chain(3, NEXT)
-    chain(4, FAR)
+    chain(4, NEAR)
     with mark("xd_fwd0"):
         cx_forward(0)
     cx_send(3)
@@ -567,6 +568,7 @@
         ag_forward(1, 2)
     with mark("xe_fwd1"):
         cx_forward(1)
+    chain(4, FAR)
     with mark("xf_agp2"):
         ag_partner(2)
 
@@ -675,21 +677,21 @@
         out_block(2)
     with mark("ye_second1"):
         second(1)
+    with mark("y_out3"):
+        out_block(3)
     with mark("yg_agf30"):
         ag_forward(3, 0)
-    with mark("y_out3"):
-        out_block(3)
+    with mark("ye_second2"):
+        second(2)
     with mark("yh_agf31"):
         ag_forward(3, 1)
-    with mark("ye_second2"):
-        second(2)
-    with mark("yk_agf32"):
-        ag_forward(3, 2)
     with mark("yf_agp1"):
         ag_partner(1)
     with mark("ye_second3"):
         second(3)
         ahead(n - 1)
+    with mark("yk_agf32"):
+        ag_forward(3, 2)
     with mark("yi_chainend4"):
         chain_end(4)
     with mark("yj_mix2"):
@@ -708,30 +710,69 @@
             device_id=(lax.rem(t + d, n), z), device_id_type=MESH,
         )
 
-    def grad_copy(m, d):
-        to = lax.rem(t + d, n)
+    edge, middle = jnp.where(lower, 0, nz - 1), jnp.where(lower, 1, nz - 2)
+    far_edge, far_middle = nz - 1 - edge, nz - 1 - middle
+    beside = jnp.where(inner, edge, middle)
+
+    def term(zz):
+        return dot(cott[at_rows(zz, rows), :], ctx2s[...])
+
+    def grad_copy(index, slot, to, to_z):
         return pltpu.make_async_remote_copy(
-            src_ref=gsend.at[m, at_rows(to, part), :],
-            dst_ref=grecv.at[m, :, at_cols(t)],
+            src_ref=gsend.at[index, at_rows(to, part), :],
+            dst_ref=grecv.at[slot, :, at_cols(t)],
             send_sem=GRAD, recv_sem=GRAD_IN,
-            device_id=(to, flip(z, m) if m else z), device_id_type=MESH,
+            device_id=(to, to_z), device_id_type=MESH,
         )
 
-    with mark("z_terms"):
-        for m in (3, 2, 1, 0):
-            zz = flip(z, m) if m else z
-            gsend[m] = dot(cott[at_rows(zz, rows), :], ctx2s[...]).astype(jnp.bfloat16)
-            for d in range(1 if m == 0 else 0, n):
-                grad_copy(m, d).start()
-        grecv[0, :, at_cols(t)] = gsend[0, at_rows(t, part), :]
+    def halves_of(h):
+        return pl.ds(h * half, half)
+
+    with mark("yz_back"):
         for d in range(1, n):
             back_copy(d).start()
         ctx2[:, at_cols(t)] = ctx2s[at_rows(t, fr), :]
+    with mark("z_terms"):
+        for index, to_z in enumerate((far_edge, far_middle)):
+            value = term(to_z)
+            fsum[index] = value
+            gsend[index] = value.astype(jnp.bfloat16)
+
+            @pl.when(~inner)
+            def _():
+                for h in range(2):
+                    pltpu.make_async_remote_copy(
+                        src_ref=gsend.at[index, halves_of(h), :],
+                        dst_ref=pbuf.at[index, halves_of(h), :],
+                        send_sem=GRAD, recv_sem=pre_sem.at[2 * index + h],
+                        device_id=(t, middle), device_id_type=MESH,
+                    ).start()
+
+        gsend[2] = term(beside).astype(jnp.bfloat16)
+        for d in range(n):
+            grad_copy(2, 1, lax.rem(t + d, n), beside).start()
+        gsend[3] = term(z).astype(jnp.bfloat16)
+        for d in range(1, n):
+            grad_copy(3, 0, lax.rem(t + d, n), z).start()
+        grecv[0, :, at_cols(t)] = gsend[3, at_rows(t, part), :]
+    with mark("za_pre"):
+        @pl.when(inner)
+        def _():
+            for index, to_z in enumerate((far_edge, far_middle)):
+                for h in range(2):
+                    view = pbuf.at[index, halves_of(h), :]
+                    received(pre_sem.at[2 * index + h], view)
+                    gsend[index, halves_of(h), :] = (
+                        fsum[index, halves_of(h), :] + view[...].astype(jnp.float32)
+                    ).astype(jnp.bfloat16)
+                    for d in range(n // 2):
+                        grad_copy(index, 2, h * (n // 2) + lax.rem(t + d, n // 2), to_z).start()
+
     with mark("za_grads"):
-        received(GRAD_IN, ctx2s.at[0 : (n * nz - 1) * part, :])
+        received(GRAD_IN, ctx2s.at[0 : (3 * n - 1) * part, :])
         total = grecv[0].astype(jnp.float32)
-        for m in range(1, nz):
-            total = total + grecv[m].astype(jnp.float32)
+        for slot in (1, 2):
+            total = total + grecv[slot].astype(jnp.float32)
         grad_ref[...] = total
     with mark("zb_back"):
         received(BACK_IN, ctx2.at[:, 0 : (n - 1) * cols])
@@ -808,7 +849,9 @@
             pltpu.VMEM((span, cols), bf16),
             pltpu.VMEM((fr, width), bf16),
             pltpu.VMEM((nz, rows, cols), bf16),
-            pltpu.VMEM((nz, rows // n, width), bf16),
+            pltpu.VMEM((3, rows // n, width), bf16),
+            pltpu.VMEM((2, rows, cols), f32),
+            pltpu.VMEM((2, rows, cols), bf16),
             dma((7,)),
             dma((4,)),
             dma((30,)),
@@ -817,6 +860,7 @@
             dma((n // 2,)),
             dma((7,)),
             pltpu.SemaphoreType.REGULAR,
+            dma((4,)),
         ],
         compiler_params=pltpu.CompilerParams(
             collective_id=0, has_side_effects=True, vmem_limit_bytes=44 * 1024 * 1024

time: 57.2 us -> 55.6 us (0.972)
  Pallas kernels: 55.1 us -> 53.5 us
    pallas_call x1, Pallas kernels: 54.4 us -> 52.7 us  [by_heads(): pl.pallas_call(functools.partial(heads_kernel, n, nz), out_shape=(jax.Sha...]
where the time goes in v3:
time: 55.6 us; the launch traced here: 55.4 us
  Pallas kernels  53.5 us (96%)
  between operations  1.93 us (3%)
    pallas_call x1, Pallas kernels, by_heads(): pl.pallas_call(functools.partial(heads_kernel, n, nz), out_shape=(jax.Sha...  52.7 us

profile of v3, /device:TPU:0, one launch (start us, length us, event | category | flops | bytes accessed | tf_op | source)
XLA Modules:
  0.0 55.4 jit_solution(17773850129303203276)
XLA Ops:
  1.9 52.7 %shard_map.104 = (bf16[128,1024]{1,0:T(8,128)(2,1)S(1)}, f32[32,1024]{1,0:T(8,128)S(1)}) custom-call(bf16[128,1024]{1,0:T(8,128)(2,1)} %bitcast.5, f32[1,1024]{1,0:T(1,128)} %bitcast.7, bf16[256,3072]{1,0:T(8,128)(2,1)} %qkv_one_ref.1, bf16[256,1024]{1,0:T(8,128)(2,1)} %out_one_ref.1, f32[1,1024]{1,0:T(1,128)} %bitcast.8, bf16[256,3072]{1,0:T(8,128)(2,1)} %qkv_two_ref.1, ...), custom_call_target="tpu_custom_call" | custom-call | tf_op jit(solution)/shard_map/pallas_call | solution.py:822
  54.7 0.8 %shard_map.105 = (bf16[128,1024]{1,0:T(8,128)(2,1)}, f32[32,1024]{1,0:T(8,128)}) custom-call(bf16[128,1024]{1,0:T(8,128)(2,1)S(1)} %get-tuple-element.6.context_ref, f32[32,1024]{1,0:T(8,128)S(1)} %get-tuple-element.7.grad_ref), custom_call_target="tpu_custom_call" | custom-call | tf_op jit(solution)/shard_map/pallas_call | solution.py:869

commit v4 on v3

--- a/solution.py
+++ b/solution.py
@@ -262,7 +262,7 @@
                     for h in pieces(which):
                         chain_wait(which, jnp.clip(there, 0, nz - 1), h)
 
-    early = width * 5 // 8
+    early = width * 3 // 8
 
     def ag_view(which, index, piece):
         if which == 0:
@@ -513,10 +513,6 @@
     with mark("v_chainend2"):
         chain_end(2)
     chain(3, FAR)
-    with mark("w_projv"):
-        for pair in range(groups):
-            project(nbuf, w1, pair, None, (v1a, v1b))
-
     def cx_copy(g, m):
         to = flip(t, (m, 4, 2)[max(m - 5, 0)])
         if m < 6:
@@ -551,6 +547,7 @@
 
     with mark("x_mix"):
         for g in range(groups):
+            project(nbuf, w1, g, None, (v1a, v1b))
             causal_mix(2 * g)
             causal_mix(2 * g + 1)
             if g < 3:
@@ -685,6 +682,11 @@
         second(2)
     with mark("yh_agf31"):
         ag_forward(3, 1)
+    with mark("yi_chainend4"):
+        chain_end(4)
+    with mark("yi_projv"):
+        for g in range(groups - 1):
+            project(nbuf2, w2, g, None, (v2a, v2b))
     with mark("yf_agp1"):
         ag_partner(1)
     with mark("ye_second3"):
@@ -692,11 +694,8 @@
         ahead(n - 1)
     with mark("yk_agf32"):
         ag_forward(3, 2)
-    with mark("yi_chainend4"):
-        chain_end(4)
     with mark("yj_mix2"):
-        for g in range(groups):
-            project(nbuf2, w2, g, None, (v2a, v2b))
+        project(nbuf2, w2, groups - 1, None, (v2a, v2b))
         for b in range(n):
             ahead_mix(b)
     with mark("yl_agp3"):

time: 55.6 us -> 55 us (0.989)
  Pallas kernels: 53.5 us -> 52.9 us
where the time goes in v4:
time: 55 us; the launch traced here: 54.9 us
  Pallas kernels  52.9 us (96%)
  between operations  1.93 us (4%)
    pallas_call x1, Pallas kernels, by_heads(): pl.pallas_call(functools.partial(heads_kernel, n, nz), out_shape=(jax.Sha...  52.2 us

profile of v4, /device:TPU:0, one launch (start us, length us, event | category | flops | bytes accessed | tf_op | source)
XLA Modules:
  0.0 54.9 jit_solution(4696270198475613162)
XLA Ops:
  1.9 52.2 %shard_map.104 = (bf16[128,1024]{1,0:T(8,128)(2,1)S(1)}, f32[32,1024]{1,0:T(8,128)S(1)}) custom-call(bf16[128,1024]{1,0:T(8,128)(2,1)} %bitcast.5, f32[1,1024]{1,0:T(1,128)} %bitcast.7, bf16[256,3072]{1,0:T(8,128)(2,1)} %qkv_one_ref.1, bf16[256,1024]{1,0:T(8,128)(2,1)} %out_one_ref.1, f32[1,1024]{1,0:T(1,128)} %bitcast.8, bf16[256,3072]{1,0:T(8,128)(2,1)} %qkv_two_ref.1, ...), custom_call_target="tpu_custom_call" | custom-call | tf_op jit(solution)/shard_map/pallas_call | solution.py:821
  54.1 0.8 %shard_map.105 = (bf16[128,1024]{1,0:T(8,128)(2,1)}, f32[32,1024]{1,0:T(8,128)}) custom-call(bf16[128,1024]{1,0:T(8,128)(2,1)S(1)} %get-tuple-element.6.context_ref, f32[32,1024]{1,0:T(8,128)S(1)} %get-tuple-element.7.grad_ref), custom_call_target="tpu_custom_call" | custom-call | tf_op jit(solution)/shard_map/pallas_call | solution.py:868
